TPU v7x, 256 devices: a whole 4x4x8 slice. The times are simulated.
256 devices in a mesh: branch: 2 (over core), gi: 16 (over y_hi, z), gj: 8 (over x, y_lo).
Axes of the slice: x: 4, y: 4 (y_hi: 2, y_lo: 2; y = y_hi * 2 + y_lo), z: 8, core: 2. Of those that a mesh axis runs over, the one named last changes fastest.
Arguments:
- homolog_embedding: float32 [128, 256, 256], P(('branch', 'gj'), 'gi'), may hold values from -6 to 6
- pair_input_tensor: float32 [256, 256, 128], P('gi', ('branch', 'gj')), may hold values from -6 to 6
- layernorm_scales: float32 [4, 256], replicated, may hold values from 0.5 to 1.5
- pair_norm_gains: float32 [3, 128], replicated, may hold values from 0.5 to 1.5
- pair_bias_matrix: float32 [128, 8], replicated
- horizontal_qkvg_kernel: float32 [256, 1024], replicated, may hold values from -0.375 to 0.375
- horizontal_final_kernel: float32 [256, 256], replicated, may hold values from -0.375 to 0.375
- vertical_qkvg_kernel: float32 [256, 1024], replicated, may hold values from -0.375 to 0.375
- vertical_final_kernel: float32 [256, 256], replicated, may hold values from -0.375 to 0.375
- feedforward_expand_kernel: float32 [256, 1024], replicated, may hold values from -0.375 to 0.375
- feedforward_shrink_kernel: float32 [1024, 256], replicated, may hold values from -0.1875 to 0.1875
- dyadic_sides_kernel: float32 [256, 64], replicated, may hold values from -0.375 to 0.375
- outer_output_matrix: float32 [1024, 128], replicated, may hold values from -1 to 1
- triangle_input_matrix: float32 [128, 640], replicated, may hold values from -0.5 to 0.5
- triangle_output_matrix: float32 [128, 128], replicated, may hold values from -0.5 to 0.5
Outputs:
- alignment_output: float32 [128, 256, 256], P(('branch', 'gj'), 'gi')
- pair_output_tensor: float32 [256, 256, 128], P('gi', ('branch', 'gj'))
All inputs are finite; a program needn't handle non-finite values.
Results may differ from a plain program's by a relative error of at most 0.0003.
Values sent between devices are 32-bit elements; how exact they have to be, the bound alone decides.
A program may use at most 64 MiB of HBM per device.

v0:
```python
import math

import jax
import jax.numpy as jnp
from jax import lax
from jax.sharding import PartitionSpec as P

epsilon = 1e-05
highest = lax.Precision.HIGHEST
lowest_start = -1e30


def from_root(shard, axis, root):
    mine = lax.axis_index(axis) == root
    return lax.psum(jnp.where(mine, shard, jnp.zeros_like(shard)), axis)


def layer_normalise(values, norm_gain):
    average = jnp.mean(values, axis=-1, keepdims=True)
    centred = values - average
    variance = jnp.mean(centred * centred, axis=-1, keepdims=True)
    return centred * lax.rsqrt(variance + epsilon) * norm_gain


def apply_projection(values, weight):
    return jnp.einsum("...c,cd->...d", values, weight, precision=highest)


def transition_update(values, norm_gain, feedforward_expand_kernel, feedforward_shrink_kernel):
    expanded = jax.nn.relu(
        apply_projection(layer_normalise(values, norm_gain), feedforward_expand_kernel)
    )
    return values + apply_projection(expanded, feedforward_shrink_kernel)


def online_update(state_carry, scores, values, einsum_form):
    running_max, sum_weights, numerator = state_carry
    new_max = jnp.maximum(running_max, jnp.max(scores, axis=-1))
    weights = jnp.exp(scores - new_max[..., None])
    sum_weights = jnp.sum(weights, axis=-1)
    numerator = jnp.einsum(einsum_form, weights, values, precision=highest)
    return (new_max, sum_weights, numerator)


def empty_state(leading, head_size):
    return (
        jnp.full(leading, lowest_start, jnp.float32),
        jnp.zeros(leading, jnp.float32),
        jnp.zeros(leading + (head_size,), jnp.float32),
    )


def panels(first_local, second_local):
    groups = lax.axis_size("gi") // lax.axis_size(("branch", "gj"))
    col_index = lax.axis_index(("branch", "gj"))
    first_panel, second_panel = (
        lax.all_gather(first_local, ("branch", "gj"), axis=1, tiled=True),
        lax.all_gather(second_local, ("branch", "gj"), axis=1, tiled=True),
    )
    pieces = from_root(second_panel, "gi", col_index * groups + 0)
    return (first_panel, pieces)


def per_device(
    homolog_embedding,
    pair_input_tensor,
    layernorm_scales,
    pair_norm_gains,
    pair_bias_matrix,
    horizontal_qkvg_kernel,
    horizontal_final_kernel,
    vertical_qkvg_kernel,
    vertical_final_kernel,
    feedforward_expand_kernel,
    feedforward_shrink_kernel,
    dyadic_sides_kernel,
    outer_output_matrix,
    triangle_input_matrix,
    triangle_output_matrix,
):
    rows_per_device, residues_per_device, alignment_width = homolog_embedding.shape
    pair_cols, pair_width = (pair_input_tensor.shape[1], pair_input_tensor.shape[2])
    head_count = pair_bias_matrix.shape[1]
    inner_feature_width = horizontal_final_kernel.shape[0]
    head_size = inner_feature_width // head_count
    outer_width = dyadic_sides_kernel.shape[1] // 2
    bias_local = apply_projection(
        layer_normalise(pair_input_tensor, pair_norm_gains[0]), pair_bias_matrix
    ).reshape(residues_per_device, pair_cols * head_count)
    bias_rows = lax.all_gather(bias_local, ("branch", "gj"), axis=1, tiled=True).reshape(
        residues_per_device, -1, head_count
    )
    bias_heads = jnp.transpose(bias_rows, (2, 0, 1))
    alignment_normalised = layer_normalise(homolog_embedding, layernorm_scales[0])
    row_query_values = apply_projection(
        alignment_normalised, horizontal_qkvg_kernel[:, :inner_feature_width]
    ).reshape(rows_per_device, residues_per_device, head_count, head_size)
    row_gate_values = apply_projection(
        alignment_normalised, horizontal_qkvg_kernel[:, 3 * inner_feature_width :]
    )
    row_start = empty_state((rows_per_device, head_count, residues_per_device), head_size)
    row_pair_slice = apply_projection(
        alignment_normalised,
        horizontal_qkvg_kernel[:, inner_feature_width : 3 * inner_feature_width],
    )
    pieces = (
        lax.all_gather(row_pair_slice[..., :inner_feature_width], "gi", axis=1, tiled=True),
        lax.all_gather(row_pair_slice[..., inner_feature_width:], "gi", axis=1, tiled=True),
    )
    key_flat = pieces[0]
    block_rows = key_flat.shape[1]
    key_block = key_flat.reshape(rows_per_device, block_rows, head_count, head_size)
    value_block = pieces[1].reshape(rows_per_device, block_rows, head_count, head_size)
    scores = (
        jnp.einsum("sihd,sjhd->shij", row_query_values, key_block, precision=highest)
        / math.sqrt(head_size)
        + bias_heads[None]
    )
    row_state = online_update(row_start, scores, value_block, "shij,sjhd->shid")
    row_heads = row_state[2] / row_state[1][..., None]
    row_attention_result = jnp.transpose(row_heads, (0, 2, 1, 3)).reshape(
        rows_per_device, residues_per_device, inner_feature_width
    )
    alignment_after_rows = homolog_embedding + apply_projection(
        jax.nn.sigmoid(row_gate_values) * row_attention_result, horizontal_final_kernel
    )
    column_normalised = layer_normalise(alignment_after_rows, layernorm_scales[1])
    column_query = apply_projection(
        column_normalised, vertical_qkvg_kernel[:, :inner_feature_width]
    ).reshape(rows_per_device, residues_per_device, head_count, head_size)
    column_pairs = apply_projection(
        column_normalised, vertical_qkvg_kernel[:, inner_feature_width : 3 * inner_feature_width]
    )
    column_gate_values = apply_projection(
        column_normalised, vertical_qkvg_kernel[:, 3 * inner_feature_width :]
    )
    column_start = empty_state((residues_per_device, head_count, rows_per_device), head_size)
    pieces = (
        lax.all_gather(
            column_pairs[..., :inner_feature_width], ("branch", "gj"), axis=0, tiled=True
        ),
        lax.all_gather(
            column_pairs[..., inner_feature_width:], ("branch", "gj"), axis=0, tiled=True
        ),
    )
    block_rows = pieces[0].shape[0]
    key_block = pieces[0].reshape(block_rows, residues_per_device, head_count, head_size)
    value_block = pieces[1].reshape(block_rows, residues_per_device, head_count, head_size)
    scores = jnp.einsum("sihd,tihd->ihst", column_query, key_block, precision=highest) / math.sqrt(
        head_size
    )
    column_state = online_update(column_start, scores, value_block, "ihst,tihd->ihsd")
    column_heads = column_state[2] / column_state[1][..., None]
    column_attention_result = jnp.transpose(column_heads, (2, 0, 1, 3)).reshape(
        rows_per_device, residues_per_device, inner_feature_width
    )
    alignment_after_columns = alignment_after_rows + apply_projection(
        jax.nn.sigmoid(column_gate_values) * column_attention_result, vertical_final_kernel
    )
    alignment_output = transition_update(
        alignment_after_columns,
        layernorm_scales[2],
        feedforward_expand_kernel,
        feedforward_shrink_kernel,
    )
    factor_pair = apply_projection(
        layer_normalise(alignment_output, layernorm_scales[3]), dyadic_sides_kernel
    )
    left_local = jnp.transpose(factor_pair[..., :outer_width], (1, 0, 2)).reshape(
        residues_per_device, rows_per_device * outer_width
    )
    right_local = jnp.transpose(factor_pair[..., outer_width:], (1, 0, 2)).reshape(
        residues_per_device, rows_per_device * outer_width
    )
    left_panel, right_panel = panels(left_local, right_local)
    all_rows = left_panel.shape[1] // outer_width
    left_three = left_panel.reshape(residues_per_device, all_rows, outer_width)
    right_three = right_panel.reshape(pair_cols, all_rows, outer_width)
    outer = jnp.einsum("isc,jsd->ijcd", left_three, right_three, precision=highest) / all_rows
    pair_first = pair_input_tensor + apply_projection(
        outer.reshape(residues_per_device, pair_cols, outer_width * outer_width),
        outer_output_matrix,
    )
    projected_values = apply_projection(
        layer_normalise(pair_first, pair_norm_gains[1]), triangle_input_matrix
    )
    left_tri = (
        jax.nn.sigmoid(projected_values[..., pair_width : 2 * pair_width])
        * projected_values[..., :pair_width]
    )
    right_tri = (
        jax.nn.sigmoid(projected_values[..., 3 * pair_width : 4 * pair_width])
        * projected_values[..., 2 * pair_width : 3 * pair_width]
    )
    out_gate = projected_values[..., 4 * pair_width :]
    left_rows, right_rows = panels(
        left_tri.reshape(residues_per_device, pair_cols * pair_width),
        right_tri.reshape(residues_per_device, pair_cols * pair_width),
    )
    left_rows = left_rows.reshape(residues_per_device, -1, pair_width)
    right_rows = right_rows.reshape(pair_cols, -1, pair_width)
    product = jnp.einsum("ikc,jkc->ijc", left_rows, right_rows, precision=highest)
    pair_output_tensor = pair_first + jax.nn.sigmoid(out_gate) * apply_projection(
        layer_normalise(product, pair_norm_gains[2]), triangle_output_matrix
    )
    return (alignment_output, pair_output_tensor)


def solution(mesh):
    return jax.shard_map(
        per_device,
        mesh=mesh,
        in_specs=(
            P(("branch", "gj"), "gi", None),
            P("gi", ("branch", "gj"), None),
            P(),
            P(),
            P(),
            P(),
            P(),
            P(),
            P(),
            P(),
            P(),
            P(),
            P(),
            P(),
            P(),
        ),
        out_specs=(P(("branch", "gj"), "gi", None), P("gi", ("branch", "gj"), None)),
        check_vma=False,
    )
```

profile of v0, /device:TPU:1, one launch (start us, length us, event | category | flops | bytes accessed | tf_op | source)
XLA Modules:
  0.0 730.1 jit_solution(3773819482061920002)
XLA Ops:
  17.5 42.5 %all_gather.28 = f32[16,2048]{0,1:T(8,128)S(1)} all-gather(f32[16,128]{0,1:T(8,128)S(1)} %convolution_bitcast_fusion.2), channel_id=1, replica_groups=mesh['branch'=2,'gi'=16,'gj'=8] {'branch','gj'}, dimensions={1}, use_global_device_ids=true | all-gather | bytes 139264 | tf_op jit(solution)/shard_map/all_gather | solution.py:90
  60.3 39.3 %all-gather.7.cloned.1.call-done = f32[8,256,256]{2,1,0:T(8,128)} async-done(((f32[8,16,256]{2,1,0:T(8,128)}), f32[8,256,256]{2,1,0:T(8,128)}) %all-gather.7.cloned.1.call-update) | async-done | bytes 2097168 | tf_op jit(solution)/shard_map/all_gather | solution.py:107
  99.6 2.9 copy.90
  102.5 2.9 fusion.101
  105.9 79.0 %all-gather.9.cloned.1.call-done = f32[8,256,256]{2,1,0:T(8,128)} async-done(((f32[8,16,256]{2,1,0:T(8,128)}), f32[8,256,256]{2,1,0:T(8,128)}) %all-gather.9.cloned.1.call-update) | async-done | bytes 2097168 | tf_op jit(solution)/shard_map/all_gather | solution.py:108
  184.9 2.9 copy.94
  187.8 3.5 fusion.1
  197.8 35.0 %all-gather.11.cloned.1.call-done = f32[128,16,256]{2,1,0:T(8,128)} async-done(((f32[8,16,256]{2,1,0:T(8,128)}), f32[128,16,256]{2,1,0:T(8,128)}) %all-gather.11.cloned.1.call-update) | async-done | bytes 2097168 | tf_op jit(solution)/shard_map/all_gather | solution.py:139
  234.9 3.2 fusion.103
  239.2 32.4 %all-gather.13.cloned.1.call-done = f32[128,16,256]{2,1,0:T(8,128)} async-done(((f32[8,16,256]{2,1,0:T(8,128)}), f32[128,16,256]{2,1,0:T(8,128)}) %all-gather.13.cloned.1.call-update) | async-done | bytes 2097168 | tf_op jit(solution)/shard_map/all_gather | solution.py:142
  273.6 4.5 fusion.2
  282.8 29.5 %all_gather.32 = f32[16,4096]{1,0:T(8,128)S(1)} all-gather(f32[16,256]{1,0:T(8,128)S(1)} %reshape.171), channel_id=1, replica_groups=mesh['branch'=2,'gi'=16,'gj'=8] {'branch','gj'}, dimensions={1}, use_global_device_ids=true | all-gather | bytes 278528 | tf_op jit(solution)/shard_map/all_gather | solution.py:58
  313.8 28.6 %all_gather.33 = f32[16,4096]{1,0:T(8,128)S(1)} all-gather(f32[16,256]{1,0:T(8,128)S(1)} %reshape.173), channel_id=1, replica_groups=mesh['branch'=2,'gi'=16,'gj'=8] {'branch','gj'}, dimensions={1}, use_global_device_ids=true | all-gather | bytes 278528 | tf_op jit(solution)/shard_map/all_gather | solution.py:57
  342.8 115.5 %all-reduce.3.cloned.1.call-done = f32[16,128,32]{1,2,0:T(8,128)} async-done(((f32[16,128,32]{1,2,0:T(8,128)}), f32[16,128,32]{1,2,0:T(8,128)}) %all-reduce.3.cloned.1.call-update) | async-done | bytes 262160 | tf_op jit(solution)/shard_map/psum | solution.py:15
  458.3 5.9 multiply_bitcast_fusion
  464.2 5.4 copy.104
  469.5 3.8 reshape.175
  477.9 44.0 %all-gather.15.cloned.1.call-done = f32[16,32768]{1,0:T(8,128)} async-done(((f32[16,2048]{1,0:T(8,128)}), f32[16,32768]{1,0:T(8,128)}) %all-gather.15.cloned.1.call-update) | async-done | bytes 2097168 | tf_op jit(solution)/shard_map/all_gather | solution.py:58
  522.4 2.1 copy.105
  524.5 35.6 %all-gather.17.cloned.1.call-done = f32[16,32768]{1,0:T(8,128)} async-done(((f32[16,2048]{1,0:T(8,128)}), f32[16,32768]{1,0:T(8,128)}) %all-gather.17.cloned.1.call-update) | async-done | bytes 2097168 | tf_op jit(solution)/shard_map/all_gather | solution.py:57
  560.2 3.3 copy.122
  563.5 2.2 copy.106
  565.8 149.1 %all-reduce.5.cloned.1.call-done = f32[16,256,128]{1,0,2:T(8,128)} async-done(((f32[16,256,128]{1,0,2:T(8,128)}), f32[16,256,128]{1,0,2:T(8,128)}) %all-reduce.5.cloned.1.call-update) | async-done | bytes 2097168 | tf_op jit(solution)/shard_map/psum | solution.py:15
  714.8 4.6 bitcast_reduce_fusion
  (124 shorter events, 37.7 us)
Async XLA Ops:
  7.2 273.4 %copy-start = (f32[256,1024]{1,0:T(8,128)S(1)}, f32[256,1024]{1,0:T(8,128)}, u32[]{:S(2)}) copy-start(f32[256,1024]{1,0:T(8,128)} %param.24) | copy-start | bytes 3145732
  7.2 6.9 copy-start.2
  7.2 6.7 copy-start.4
  7.2 8.5 %copy-start.15 = (f32[3,128]{1,0:T(4,128)S(1)}, f32[3,128]{1,0:T(4,128)}, u32[]{:S(2)}) copy-start(f32[3,128]{1,0:T(4,128)} %param.18) | copy-start | bytes 4612
  7.2 9.3 %copy-start.13 = (f32[128,8]{0,1:T(8,128)S(1)}, f32[128,8]{0,1:T(8,128)}, u32[]{:S(2)}) copy-start(f32[128,8]{0,1:T(8,128)} %param.19) | copy-start | bytes 12292
  7.2 92.4 %all-gather.7.cloned.1.call-start = ((), (), s32[]{:S(2)}) async-start(), calls=%async_computation | async-start | bytes 2228224 | tf_op jit(solution)/shard_map/all_gather | solution.py:107
  13.1 171.8 %all-gather.9.cloned.1.call-start = ((), (), s32[]{:S(2)}) async-start(), calls=%async_computation.1 | async-start | bytes 2228224 | tf_op jit(solution)/shard_map/all_gather | solution.py:108
  13.9 219.0 %all-gather.11.cloned.1.call-start = ((), (), s32[]{:S(2)}) async-start(), calls=%async_computation.2 | async-start | bytes 2228224 | tf_op jit(solution)/shard_map/all_gather | solution.py:139
  191.4 3.2 copy-start.7
  195.7 75.8 %all-gather.13.cloned.1.call-start = ((), (), s32[]{:S(2)}) async-start(), calls=%async_computation.3 | async-start | bytes 2228224 | tf_op jit(solution)/shard_map/all_gather | solution.py:142
  196.3 262.0 %all-reduce.3.cloned.1.call-start = ((), (), s32[]{:S(2)}) async-start(), calls=%async_computation.4 | async-start | bytes 524288 | tf_op jit(solution)/shard_map/psum | solution.py:15
  278.1 1.9 copy-start.10
  278.1 2.5 copy-start.12
  278.2 3.2 copy-start.6
  280.4 1.9 copy-start.11
  282.1 31.6 %copy-start.5 = (f32[8,16,256]{2,1,0:T(8,128)}, f32[8,16,256]{2,1,0:T(8,128)S(1)}, u32[]{:S(2)}) copy-start(f32[8,16,256]{2,1,0:T(8,128)S(1)} %get-tuple-element.26) | copy-start | bytes 393220
  313.7 208.2 %all-gather.15.cloned.1.call-start = ((), (), s32[]{:S(2)}) async-start(), calls=%async_computation.5 | async-start | bytes 2228224 | tf_op jit(solution)/shard_map/all_gather | solution.py:58
  469.5 3.8 copy-start.8
  469.5 5.1 copy-start.14
  473.3 1.3 copy-start.9
  477.1 83.1 %all-gather.17.cloned.1.call-start = ((), (), s32[]{:S(2)}) async-start(), calls=%async_computation.7 | async-start | bytes 2228224 | tf_op jit(solution)/shard_map/all_gather | solution.py:57
  477.9 237.0 %all-reduce.5.cloned.1.call-start = ((), (), s32[]{:S(2)}) async-start(), calls=%async_computation.6 | async-start | bytes 4194304 | tf_op jit(solution)/shard_map/psum | solution.py:15
  565.8 155.6 %copy-start.16 = (f32[128]{0:T(128)S(1)}, f32[128]{0:T(128)}, u32[]{:S(2)}) copy-start(f32[128]{0:T(128)} %get-tuple-element.14) | copy-start | bytes 1540
  565.8 155.6 %copy-start.17 = (f32[128,128]{1,0:T(8,128)S(1)}, f32[128,128]{1,0:T(8,128)}, u32[]{:S(2)}) copy-start(f32[128,128]{1,0:T(8,128)} %param.29) | copy-start | bytes 196612
  (2 other events, 1.7 us)
Sparse Core Ops, SparseCore 0:
  13.3 86.3 all-gather.6
  102.8 82.0 all-gather.8
  195.9 36.9 all-gather.10
  235.2 36.3 all-gather.12
  313.8 144.4 all-reduce.2
  477.2 44.6 all-gather.14
  523.7 36.3 all-gather.16
  562.8 151.9 all-reduce.4
where the time goes:
time: 741 us; the launch traced here: 730 us
  waiting for transfers between devices  531 us (72%)
  blocking collectives  101 us (14%)
  local copies, waits for them, and re-layouts  39.3 us (5%)
  matrix products  39.2 us (5%)
  between operations  14.8 us (2%)
    psum x2, waiting for transfers between devices, from_root(): return lax.psum(jnp.where(mine, shard, jnp.zeros_like(shard)), axis)  265 us
    all_gather x1, waiting for transfers between devices, per_device(): lax.all_gather(row_pair_slice[..., inner_feature_width:], 'gi', axis=1, t...  79 us
    all_gather x1, waiting for transfers between devices, panels(): lax.all_gather(second_local, ('branch', 'gj'), axis=1, tiled=True)  44 us
    all_gather x1, blocking collectives, per_device(): lax.all_gather(bias_local, ('branch', 'gj'), axis=1, tiled=True)  42.5 us
    all_gather x1, waiting for transfers between devices, per_device(): lax.all_gather(row_pair_slice[..., :inner_feature_width], 'gi', axis=1, t...  39.3 us
    all_gather x1, waiting for transfers between devices, panels(): lax.all_gather(first_local, ('branch', 'gj'), axis=1, tiled=True)  35.6 us
    all_gather x1, waiting for transfers between devices, per_device(): lax.all_gather(column_pairs[..., :inner_feature_width], ('branch', 'gj'),...  35 us
    all_gather x1, waiting for transfers between devices, per_device(): lax.all_gather(column_pairs[..., inner_feature_width:], ('branch', 'gj'),...  32.4 us
  transfers between devices with their start and end apart: 8, of which 8 were waited for; matrix products, arithmetic and copies ran while one was open for 4% of the time, Pallas kernels for 0%

commit v1 on v0

v1 whole, which is shorter than its diff:
```python
import functools
import math

import jax
import jax.numpy as jnp
from jax import lax
from jax.experimental import pallas as pl
from jax.experimental.pallas import tpu as pltpu
from jax.sharding import PartitionSpec as P

F32, BF16 = jnp.float32, jnp.bfloat16
NN = (((1,), (0,)), ((), ()))
NT = (((1,), (1,)), ((), ()))
MESH = pl.DeviceIdType.MESH
EPS = 1e-05
ROOT = 1.0 / math.sqrt(32.0)


def roll(x, shift, axis):
    return pltpu.roll(x, shift, axis)


def split(x):
    hi = x.astype(BF16)
    return hi, (x - hi.astype(F32)).astype(BF16)


def dot(a, b, dims):
    return lax.dot_general(a, b, dims, preferred_element_type=F32)


def mm(a, b, dims=NN):
    return dot(a[0], b[0], dims) + (dot(a[0], b[1], dims) + dot(a[1], b[0], dims))


def norm(x, gain):
    centred = x - jnp.mean(x, axis=-1, keepdims=True)
    variance = jnp.mean(centred * centred, axis=-1, keepdims=True)
    return centred * lax.rsqrt(variance + EPS) * gain


def iota(shape, dim):
    return lax.broadcasted_iota(jnp.int32, shape, dim)


def swap_blocks(x, bits, lane_shift):
    sub, lane = iota(x.shape, 1), iota(x.shape, 2)
    for b in range(bits):
        rows, lanes = 1 << b, 1 << (lane_shift + b)
        sbit, lbit = (sub >> b) & 1, (lane >> (lane_shift + b)) & 1
        down = roll(roll(x, lanes, 2), 8 - rows, 1)
        up = roll(roll(x, 128 - lanes, 2), rows, 1)
        x = jnp.where(sbit == lbit, x, jnp.where(sbit == 0, down, up))
    return x


def f_bias(pair, gain, wb):
    wide = (iota((8, 128), 1) // 16 == iota((8, 128), 0)).astype(BF16)
    w = tuple(dot(part, wide, NN).astype(BF16) for part in split(wb))
    y = mm(split(norm(pair, gain)), w)
    y = jnp.where(iota(y.shape, 0) % 16 == iota(y.shape, 1) % 16, y, 0.0)
    return jnp.sum(y.reshape(16, 16, 128), axis=1)


def head_scores(k, q, h):
    own = iota(k[0].shape, 1) // 32 == h
    zero = jnp.zeros_like(k[0])
    return mm((jnp.where(own, k[0], zero), jnp.where(own, k[1], zero)), q, NT) * ROOT


def attend(scores, vt, h):
    weights = jnp.exp(scores - jnp.max(scores, axis=0, keepdims=True))
    total = jnp.sum(weights, axis=0, keepdims=True)
    rows = slice(32 * h, 32 * h + 32)
    return mm((vt[0][rows], vt[1][rows]), split(weights)) / total


def f_opm(left, right, wo):
    outer = (mm(split(left), split(right), NT) * (1.0 / 128.0)).reshape(16, 4, 8, 512)
    total = None
    for g in range(4):
        parts = [
            swap_blocks(outer[:, g, :, 128 * n : 128 * n + 128], 2, 5).reshape(128, 128)
            for n in range(4)
        ]
        term = mm(split(jnp.concatenate(parts, axis=0)), wo(g))
        total = term if total is None else total + term
    total = total.reshape(4, 16, 8, 256)
    halves = []
    for n in range(2):
        a, b = total[2 * n], total[2 * n + 1]
        even = a[..., :128] + roll(a[..., 128:], 4, 1)
        odd = b[..., 128:] + roll(b[..., :128], 4, 1)
        halves.append(jnp.where(iota(even.shape, 1) < 4, even, odd))
    return halves


def kernel(
    hom, pair, scales, pgains, wb, h_wq, h_wf, h_wv, h_wvf, h_we, h_ws, h_wd, h_wo, h_wt, h_wto,
    out_al, out_pair,
    wq, wf, wv, wvf, we, ws, wd, wo, wt, wto,
    bq, bf, bv, bvf, be, bs, bwd, bo, bt, bto,
    s_bias1, r_bias1, s_bias2, r_bias2, r_raw, gate, scores,
    s_att, r_att, first, s_col, r_col, s_al, r_al, s_ab, r_a, r_b,
    pf, gout, s_ta, s_tb, r_ta, r_tb, s_ba, s_bb, r_ba, r_bb, s_c, r_c, s_d, r_d,
    wsem, ssem, rsem,
):
    core, gi, gj = lax.axis_index("branch"), lax.axis_index("gi"), lax.axis_index("gj")
    bj = core * 8 + gj
    half, z = gi // 8, gi % 8

    def load(n, src, dst):
        copy = pltpu.make_async_copy(src, dst, wsem.at[n])
        copy.start()
        return copy

    loads = {"q": []}
    for b in range(4):
        column = pl.multiple_of(256 * b + 128 * half, 128)
        loads["q"].append(load(b, h_wq.at[:, pl.ds(column, 128)], wq.at[:, pl.ds(128 * b, 128)]))
    for n, (name, src, dst) in enumerate(
        (
            ("f", h_wf, wf), ("v", h_wv, wv), ("vf", h_wvf, wvf), ("e", h_we, we), ("s", h_ws, ws),
            ("d", h_wd, wd), ("o", h_wo, wo), ("t", h_wt, wt), ("to", h_wto, wto),
        )
    ):
        loads[name] = [load(4 + n, src, dst)]

    def ready(name, src, dst):
        for copy in loads[name]:
            copy.wait()
        depth = src.shape[0]

        @pl.loop(0, depth // 32)
        def _(n):
            rows = pl.ds(pl.multiple_of(n * 32, 32), 32)
            hi, lo = split(src[rows, :])
            dst[0, rows, :] = hi
            dst[1, rows, :] = lo

    def weight(ref, rows=slice(None), columns=slice(None)):
        return ref[0, rows, columns], ref[1, rows, columns]

    def on_gi(g):
        return {"gi": g}

    def on_bj(b):
        return {"branch": b // 8, "gj": b % 8}

    def cross(g):
        return {"gi": g, "branch": gi // 8, "gj": gi % 8}

    def each(count, me, one):
        @pl.loop(1, count)
        def _(d):
            one(lax.rem(me + d, count))

    def send(n, src, dst, device):
        pltpu.make_async_remote_copy(
            src_ref=src, dst_ref=dst, send_sem=ssem.at[n], recv_sem=rsem.at[n],
            device_id=device, device_id_type=MESH,
        ).start()

    def keep(n, src, dst):
        pltpu.make_async_copy(src, dst, rsem.at[n]).start()

    def exchange(n, me, device, src, dst):
        keep(n, src(me), dst)
        each(16, me, lambda peer: send(n, src(peer), dst, device(peer)))

    def eight(ref, b):
        return ref.at[:, pl.ds(pl.multiple_of(b * 8, 8), 8), :]

    def arrived(n, whole):
        pltpu.make_async_copy(whole, whole, rsem.at[n]).wait()

    def sent(n, most):
        pltpu.make_async_copy(most, most, ssem.at[n]).wait()

    barrier = pltpu.get_barrier_semaphore()

    def greet(device):
        pl.semaphore_signal(barrier, inc=1, device_id=device, device_id_type=MESH)

    each(16, gi, lambda g: greet(on_gi(g)))
    each(16, bj, lambda b: greet(on_bj(b)))
    each(16, bj, lambda b: greet({"gi": bj, "branch": b // 8, "gj": b % 8}))

    @pl.when(gi != bj)
    def _():
        greet({"gi": bj})

    pair2 = pair[...].reshape(256, 128)
    s_bias1[...] = f_bias(pair2, pgains[0:1, :], wb[...])

    pl.semaphore_wait(barrier, 45 + jnp.where(gi == bj, 0, 1))

    exchange(1, gi, on_gi, lambda g: s_bias1, r_bias1.at[gi])
    exchange(0, gi, on_gi, lambda g: hom.at[g % 8], r_raw.at[gi])
    ready("q", wq, bq)
    arrived(1, r_bias1)
    s_bias2[...] = r_bias1[...].reshape(256, 128).T.reshape(8, 16, 256)
    mine = s_bias2.at[pl.ds(half * 4, 4)]
    slot = r_bias2.at[:, pl.ds(pl.multiple_of(bj * 16, 16), 16), :]
    exchange(2, bj, on_bj, lambda b: mine, slot)

    arrived(0, r_raw)
    x = norm(r_raw[...].reshape(256, 256), scales[0:1, :])
    xs = split(x)
    q = split(mm(xs, weight(bq, columns=slice(0, 128))))
    k = split(mm(xs, weight(bq, columns=slice(128, 256))))
    vt = split(mm(xs, weight(bq, columns=slice(256, 384))).T)
    gate[...] = jax.nn.sigmoid(mm(xs, weight(bq, columns=slice(384, 512))))
    for h in range(4):
        scores[h] = head_scores(k, q, h)
    ready("f", wf, bf)
    arrived(2, r_bias2)
    heads = [attend(scores[h] + r_bias2[h], vt, h) for h in range(4)]
    att = gate[...] * jnp.concatenate(heads, axis=0).T
    s_att[...] = att.reshape(16, 16, 128)
    exchange(3, gi, on_gi, lambda g: s_att.at[g], r_att.at[gi])
    ready("v", wv, bv)
    ready("vf", wvf, bvf)

    arrived(3, r_att)
    a = r_att[...].reshape(256, 128)
    value = (
        hom[...].reshape(128, 256)
        + mm(split(a[:128]), weight(bf, slice(0, 128)))
        + mm(split(a[128:]), weight(bf, slice(128, 256)))
    )
    for n in range(2):
        lanes = slice(128 * n, 128 * n + 128)
        first[n] = value[:, lanes]
        for p in range(16):
            s_col[p, :, lanes] = first[n, pl.ds(p, 8, stride=16), :]
    exchange(4, bj, on_bj, lambda b: s_col.at[b], r_col.at[bj])
    ready("e", we, be)
    ready("s", ws, bs)

    arrived(4, r_col)
    col = r_col[...].reshape(128, 256)
    xs = split(norm(col, scales[1:2, :]))
    pieces = []
    for n in range(2):
        lanes = [slice(256 * b + 128 * n, 256 * b + 128 * n + 128) for b in range(4)]
        q = split(mm(xs, weight(bv, columns=lanes[0])))
        k = split(mm(xs, weight(bv, columns=lanes[1])))
        vt = split(mm(xs, weight(bv, columns=lanes[2])).T)
        g = jax.nn.sigmoid(mm(xs, weight(bv, columns=lanes[3])))
        heads = [attend(head_scores(k, q, h), vt, h) for h in range(4)]
        pieces.append(g * jnp.concatenate(heads, axis=0).T)
    second = (
        col
        + mm(split(pieces[0]), weight(bvf, slice(0, 128)))
        + mm(split(pieces[1]), weight(bvf, slice(128, 256)))
    )
    wide = jax.nn.relu(mm(split(norm(second, scales[2:3, :])), weight(be)))
    al = second + mm(split(wide), weight(bs))
    s_al[0], s_al[1] = al[:, :128], al[:, 128:]
    for copy in loads["d"]:
        copy.wait()
    factors = mm(split(norm(al, scales[3:4, :])), split(wd[...])).T
    s_ab[...] = factors.reshape(2, 32, 128)
    exchange(5, bj, on_bj, lambda b: s_ab.at[0], r_a.at[bj])

    @pl.loop(0, 16)
    def _(d):
        g = lax.rem(gi + d, 16)
        stays = jnp.logical_and(g == gi, gi == bj)

        @pl.when(stays)
        def _():
            keep(6, s_ab.at[1], r_b.at[bj])

        @pl.when(jnp.logical_not(stays))
        def _():
            send(6, s_ab.at[1], r_b.at[bj], cross(g))

    exchange(7, bj, on_bj, lambda b: eight(s_al, b), eight(r_al, bj))
    ready("o", wo, bo)
    ready("t", wt, bt)
    ready("to", wto, bto)

    arrived(5, r_a)
    arrived(6, r_b)

    def outer_weight(g):
        parts = [weight(bo, slice(256 * g + 128 * n, 256 * g + 128 * n + 128)) for n in range(2)]
        return tuple(jnp.concatenate([parts[0][m], parts[1][m]], axis=1) for m in range(2))

    updates = f_opm(r_a[...].reshape(512, 128), r_b[...].reshape(512, 128), outer_weight)
    for n in range(2):
        rows = slice(8 * n, 8 * n + 8)
        pf[:, rows, :] = pair[:, rows, :] + updates[n]
    xs = split(norm(pf[...].reshape(256, 128), pgains[1:2, :]))
    r = [mm(xs, weight(bt, columns=slice(128 * n, 128 * n + 128))) for n in range(5)]
    ta, tb = jax.nn.sigmoid(r[1]) * r[0], jax.nn.sigmoid(r[3]) * r[2]
    for n in range(2):
        s_ta[n] = ta[128 * n : 128 * n + 128].T
        s_tb[n] = tb[128 * n : 128 * n + 128].T
    gout[...] = jax.nn.sigmoid(r[4])

    exchange(8, bj, on_bj, lambda b: eight(s_ta, b), eight(r_ta, bj))
    exchange(9, bj, on_bj, lambda b: eight(s_tb, b), eight(r_tb, bj))

    def regroup(src, dst):
        for ih in range(2):
            for bh in range(2):
                block = jnp.stack([src[ih, pl.ds(64 * bh + c, 8, stride=8), :] for c in range(8)])
                dst[:, 8 * ih : 8 * ih + 8, 128 * bh : 128 * bh + 128] = swap_blocks(block, 3, 4)

    arrived(8, r_ta)
    regroup(r_ta, s_ba)
    exchange(10, gi, on_gi, lambda g: s_ba.at[g % 8], r_ba.at[gi])
    arrived(9, r_tb)
    regroup(r_tb, s_bb)
    keep(11, s_bb.at[z], r_bb.at[z])
    each(8, z, lambda other: send(11, s_bb.at[other], r_bb.at[z], on_gi(half * 8 + other)))
    arrived(10, r_ba)
    arrived(11, r_bb)
    x = mm(split(r_ba[...].reshape(256, 256)), split(r_bb[...].reshape(128, 256)), NT)
    s_c[...] = x.reshape(16, 16, 128)
    exchange(12, gi, on_gi, lambda g: s_c.at[g], r_c.at[gi])

    arrived(7, r_al)
    for row in range(8):
        for n in range(2):
            out_al[row, :, 128 * n : 128 * n + 128] = r_al[n, pl.ds(row, 16, stride=8), :]

    arrived(12, r_c)
    for hh in range(2):
        for ih in range(2):
            block = swap_blocks(r_c[8 * hh : 8 * hh + 8, 8 * ih : 8 * ih + 8, :], 3, 4)
            for c in range(8):
                s_d[ih, pl.ds(64 * hh + c, 8, stride=8), :] = block[c]
    exchange(13, bj, on_bj, lambda b: eight(s_d, b), eight(r_d, bj))
    arrived(13, r_d)
    x = norm(jnp.concatenate([r_d[0].T, r_d[1].T], axis=0), pgains[2:3, :])
    y = pf[...].reshape(256, 128) + gout[...] * mm(split(x), weight(bto))
    out_pair[...] = y.reshape(16, 16, 128)

    fifteen = pl.ds(0, 15)
    for n, ref in ((0, r_raw), (1, r_bias1), (3, s_att), (4, s_col), (5, r_a), (12, s_c)):
        sent(n, ref.at[fifteen])
    sent(2, r_bias2.at[:, pl.ds(0, 240), :])
    for n, ref in ((7, s_al), (8, s_ta), (9, s_tb), (13, s_d)):
        sent(n, ref.at[:, pl.ds(0, 120), :])
    sent(10, r_ba.at[fifteen])
    sent(11, r_bb.at[pl.ds(0, 7)])
    sent(6, r_b.at[fifteen])

    @pl.when(gi != bj)
    def _():
        sent(6, r_b.at[pl.ds(0, 1)])


def solution(mesh):
    def vmem(*shape, dtype=F32):
        return pltpu.VMEM(shape, dtype)

    widths = (
        (256, 512), (256, 256), (256, 1024), (256, 256), (256, 1024), (1024, 256), (256, 64),
        (1024, 128), (128, 640), (128, 128),
    )
    scratch = [vmem(*w) for w in widths] + [vmem(2, *w, dtype=BF16) for w in widths] + [
        vmem(16, 128), vmem(16, 16, 128), vmem(8, 16, 256), vmem(4, 256, 256), vmem(16, 16, 256),
        vmem(256, 128), vmem(4, 256, 256),
        vmem(16, 16, 128), vmem(16, 16, 128), vmem(2, 128, 128), vmem(16, 8, 256), vmem(16, 8, 256),
        vmem(2, 128, 128), vmem(2, 128, 128), vmem(2, 32, 128), vmem(16, 32, 128), vmem(16, 32, 128),
        vmem(16, 16, 128), vmem(256, 128), vmem(2, 128, 128), vmem(2, 128, 128), vmem(2, 128, 128), vmem(2, 128, 128),
        vmem(8, 16, 256), vmem(8, 16, 256), vmem(16, 16, 256), vmem(8, 16, 256),
        vmem(16, 16, 128), vmem(16, 16, 128), vmem(2, 128, 128), vmem(2, 128, 128),
        pltpu.SemaphoreType.DMA((13,)), pltpu.SemaphoreType.DMA((14,)), pltpu.SemaphoreType.DMA((14,)),
    ]

    def per_device(*args):
        return pl.pallas_call(
            kernel,
            out_shape=(
                jax.ShapeDtypeStruct((8, 16, 256), F32),
                jax.ShapeDtypeStruct((16, 16, 128), F32),
            ),
            in_specs=[pl.BlockSpec(memory_space=pltpu.VMEM)] * 5 + [pl.BlockSpec(memory_space=pl.ANY)] * 10,
            out_specs=(pl.BlockSpec(memory_space=pltpu.VMEM),) * 2,
            scratch_shapes=scratch,
            compiler_params=pltpu.CompilerParams(
                collective_id=0, has_side_effects=True, vmem_limit_bytes=56 * 1024 * 1024
            ),
            name="block",
        )(*args)

    msa, pairs = P(("branch", "gj"), "gi", None), P("gi", ("branch", "gj"), None)
    return jax.shard_map(
        per_device, mesh=mesh, in_specs=(msa, pairs) + (P(),) * 13, out_specs=(msa, pairs), check_vma=False
    )
```

time: 741 us -> 100 us (0.13); the launches traced: 730 us -> 100 us
  waiting for transfers between devices: 531 us -> 0 us
  blocking collectives: 101 us -> 0 us
  Pallas kernels: 0 us -> 94.8 us
  matrix products: 39.2 us -> 0 us
  local copies, waits for them, and re-layouts: 39.3 us -> 4.47 us
  between operations: 14.8 us -> 0.66 us
    all_gather x6 -> x0, waiting for transfers between devices: 265 us -> none  [the longest x1 79 us: per_device(): lax.all_gather(row_pair_slice[..., inner_feature_width:], 'gi', axis=1, t...]
    psum x2 -> x0, waiting for transfers between devices: 265 us -> none  [from_root(): return lax.psum(jnp.where(mine, shard, jnp.zeros_like(shard)), axis)]
    all_gather x3 -> x0, blocking collectives: 101 us -> none  [the longest x1 42.5 us: per_device(): lax.all_gather(bias_local, ('branch', 'gj'), axis=1, tiled=True)]
    pallas_call x0 -> x1, Pallas kernels: none -> 94.8 us  [per_device(): pl.pallas_call(kernel, out_shape=(jax.ShapeDtypeStruct((8, 16, 256), F32)...]
    dot_general x21 -> x0, matrix products: 39.2 us -> none  [the longest x15 14.6 us: apply_projection(): return jnp.einsum('...c,cd->...d', values, weight, precision=highest)]
    reshape x12 -> x0, local copies, waits for them, and re-layouts: 11.5 us -> none  [the longest x1 3.81 us: per_device(): outer.reshape(residues_per_device, pair_cols, outer_width * outer_width)]
    all_gather x4 -> x0, local copies, waits for them, and re-layouts: 9.78 us -> none  [the longest x1 2.93 us: per_device(): lax.all_gather(row_pair_slice[..., :inner_feature_width], 'gi', axis=1, t...]
  transfers between devices with their start and end apart: 8 -> 0, of which waited for: 8 -> 0; matrix products, arithmetic and copies ran while one was open for 4% -> 0% of each run, Pallas kernels for 0% -> 0%
where the time goes in v1:
time: 100 us
  Pallas kernels  94.8 us (95%)
  local copies, waits for them, and re-layouts  4.47 us (4%)
    pallas_call x1, Pallas kernels, per_device(): pl.pallas_call(kernel, out_shape=(jax.ShapeDtypeStruct((8, 16, 256), F32)...  94.8 us
    unnamed x8, local copies, waits for them, and re-layouts  4.47 us

profile of v1, /device:TPU:1, one launch (start us, length us, event | category | flops | bytes accessed | tf_op | source)
XLA Modules:
  0.0 100.0 jit_solution(14469924052641062335)
XLA Ops:
  0.6 0.0 copy-start.1
  0.6 1.4 %copy.17.wb = f32[128,8]{1,0:T(8,128)} copy(f32[128,8]{0,1:T(8,128)} %param.19) | data formatting | bytes 8192 | tf_op args[4]
  2.1 0.0 copy-done.1
  2.1 0.8 copy.18.h_wd
  2.8 94.8 %block.1 = (f32[8,16,256]{2,1,0:T(8,128)}, f32[16,16,128]{2,1,0:T(8,128)}) custom-call(f32[8,16,256]{2,1,0:T(8,128)} %hom.1, f32[16,16,128]{2,1,0:T(8,128)} %pair.1, f32[4,256]{1,0:T(4,128)} %scales.1, f32[3,128]{1,0:T(4,128)} %pgains.1, f32[128,8]{1,0:T(8,128)} %copy.17.wb, f32[256,1024]{1,0:T(8,128)} %h_wq.1, f32[256,256]{1,0:T(8,128)} %h_wf.1, ...), custom_call_target="tpu_custom_call" | custom-call | tf_op jit(solution)/shard_map/block/pallas_call | solution.py:378
  97.7 0.0 copy-start
  97.7 1.6 %copy.21 = f32[8,16,256]{2,1,0:T(8,128)} copy(f32[8,16,256]{2,1,0:T(8,128)} %get-tuple-element.4) | data formatting | bytes 262144
  99.3 0.0 copy-done
  99.3 0.7 copy.22
Async XLA Ops:
  0.6 1.5 %copy-start.1 = (f32[256,64]{0,1:T(8,128)S(1)}, f32[256,64]{0,1:T(8,128)}, u32[]{:S(2)}) copy-start(f32[256,64]{0,1:T(8,128)} %param.26) | copy-start | bytes 196612
  97.7 1.6 %copy-start = (f32[16,16,128]{2,1,0:T(8,128)S(1)}, f32[16,16,128]{2,1,0:T(8,128)}, u32[]{:S(2)}) copy-start(f32[16,16,128]{2,1,0:T(8,128)} %get-tuple-element.5) | copy-start | bytes 393220

commit v2 on v1

--- a/solution.py
+++ b/solution.py
@@ -30,7 +30,9 @@
 
 
 def mm(a, b, dims=NN):
-    return dot(a[0], b[0], dims) + (dot(a[0], b[1], dims) + dot(a[1], b[0], dims))
+    rows = a[0].shape[0]
+    both = dot(jnp.concatenate(a, axis=0), b[0], dims)
+    return both[:rows] + (dot(a[0], b[1], dims) + both[rows:])
 
 
 def norm(x, gain):
@@ -54,12 +56,15 @@
     return x
 
 
-def f_bias(pair, gain, wb):
-    wide = (iota((8, 128), 1) // 16 == iota((8, 128), 0)).astype(BF16)
-    w = tuple(dot(part, wide, NN).astype(BF16) for part in split(wb))
-    y = mm(split(norm(pair, gain)), w)
-    y = jnp.where(iota(y.shape, 0) % 16 == iota(y.shape, 1) % 16, y, 0.0)
-    return jnp.sum(y.reshape(16, 16, 128), axis=1)
+def f_bias(pair, gain, wbt):
+    lane, row = iota((256, 8), 0), iota((256, 8), 1)
+    wide = (4 * (lane // 128) + lane // 16 % 4 == row).astype(BF16)
+    w = tuple(dot(wide, part, NN).astype(BF16) for part in split(wbt))
+    y = mm(split(norm(pair, gain)), w, NT)
+    row, lane = iota(y.shape, 0), iota(y.shape, 1)
+    own = jnp.logical_and(row % 16 == lane % 16, row // 128 == lane // 64 % 2)
+    y = jnp.sum(jnp.where(own, y, 0.0).reshape(2, 8, 16, 256), axis=2)
+    return y[0] + y[1]
 
 
 def head_scores(k, q, h):
@@ -96,25 +101,57 @@
 
 
 def kernel(
-    hom, pair, scales, pgains, wb, h_wq, h_wf, h_wv, h_wvf, h_we, h_ws, h_wd, h_wo, h_wt, h_wto,
+    h_hom, h_pair, h_scales, h_pgains, h_wb, h_wq, h_wf, h_wv, h_wvf, h_we, h_ws, h_wd, h_wo, h_wt, h_wto,
     out_al, out_pair,
+    hom, pair, scales, pgains, wb,
     wq, wf, wv, wvf, we, ws, wd, wo, wt, wto,
-    bq, bf, bv, bvf, be, bs, bwd, bo, bt, bto,
+    bq, bf, bv, bvf, be, bs, bo, bt, bto,
     s_bias1, r_bias1, s_bias2, r_bias2, r_raw, gate, scores,
     s_att, r_att, first, s_col, r_col, s_al, r_al, s_ab, r_a, r_b,
     pf, gout, s_ta, s_tb, r_ta, r_tb, s_ba, s_bb, r_ba, r_bb, s_c, r_c, s_d, r_d,
-    wsem, ssem, rsem,
+    wsem, ssem, rsem, bsem,
 ):
     core, gi, gj = lax.axis_index("branch"), lax.axis_index("gi"), lax.axis_index("gj")
     bj = core * 8 + gj
     half, z = gi // 8, gi % 8
 
+    def on_gi(g):
+        return {"gi": g}
+
+    def on_bj(b):
+        return {"branch": b // 8, "gj": b % 8}
+
+    def cross(g):
+        return {"gi": g, "branch": gi // 8, "gj": gi % 8}
+
+    def each(count, me, one):
+        @pl.loop(1, count)
+        def _(d):
+            one(lax.rem(me + d, count))
+
+    barrier = pltpu.get_barrier_semaphore()
+
+    def greet(device):
+        pl.semaphore_signal(barrier, inc=1, device_id=device, device_id_type=MESH)
+
+    each(16, gi, lambda g: greet(on_gi(g)))
+    each(16, bj, lambda b: greet(on_bj(b)))
+
     def load(n, src, dst):
         copy = pltpu.make_async_copy(src, dst, wsem.at[n])
         copy.start()
         return copy
 
-    loads = {"q": []}
+    loads = {}
+    for n, (name, src, dst) in enumerate(
+        (
+            ("pair", h_pair, pair), ("pgains", h_pgains, pgains), ("b", h_wb, wb),
+            ("hom", h_hom, hom), ("scales", h_scales, scales),
+        )
+    ):
+        loads[name] = load(14 + n, src, dst)
+
+    loads["q"] = []
     for b in range(4):
         column = pl.multiple_of(256 * b + 128 * half, 128)
         loads["q"].append(load(b, h_wq.at[:, pl.ds(column, 128)], wq.at[:, pl.ds(128 * b, 128)]))
@@ -141,20 +178,6 @@
     def weight(ref, rows=slice(None), columns=slice(None)):
         return ref[0, rows, columns], ref[1, rows, columns]
 
-    def on_gi(g):
-        return {"gi": g}
-
-    def on_bj(b):
-        return {"branch": b // 8, "gj": b % 8}
-
-    def cross(g):
-        return {"gi": g, "branch": gi // 8, "gj": gi % 8}
-
-    def each(count, me, one):
-        @pl.loop(1, count)
-        def _(d):
-            one(lax.rem(me + d, count))
-
     def send(n, src, dst, device):
         pltpu.make_async_remote_copy(
             src_ref=src, dst_ref=dst, send_sem=ssem.at[n], recv_sem=rsem.at[n],
@@ -177,34 +200,46 @@
     def sent(n, most):
         pltpu.make_async_copy(most, most, ssem.at[n]).wait()
 
-    barrier = pltpu.get_barrier_semaphore()
-
-    def greet(device):
-        pl.semaphore_signal(barrier, inc=1, device_id=device, device_id_type=MESH)
-
-    each(16, gi, lambda g: greet(on_gi(g)))
-    each(16, bj, lambda b: greet(on_bj(b)))
-    each(16, bj, lambda b: greet({"gi": bj, "branch": b // 8, "gj": b % 8}))
-
-    @pl.when(gi != bj)
-    def _():
-        greet({"gi": bj})
-
-    pair2 = pair[...].reshape(256, 128)
-    s_bias1[...] = f_bias(pair2, pgains[0:1, :], wb[...])
-
-    pl.semaphore_wait(barrier, 45 + jnp.where(gi == bj, 0, 1))
-
-    exchange(1, gi, on_gi, lambda g: s_bias1, r_bias1.at[gi])
-    exchange(0, gi, on_gi, lambda g: hom.at[g % 8], r_raw.at[gi])
+    for name in ("pair", "pgains", "b"):
+        loads[name].wait()
+    bias = f_bias(pair[...].reshape(256, 128), pgains[0:1, :], wb[...])
+    s_bias1[0], s_bias1[1] = bias[:, :128], bias[:, 128:]
+    pl.semaphore_wait(barrier, 30)
+    exchange(1, gi, on_gi, lambda g: s_bias1.at[g // 8], r_bias1.at[gi])
+    loads["hom"].wait()
+    exchange(0, gi, on_gi, lambda g: hom.at[g % 8], r_raw.at[:, gi])
     ready("q", wq, bq)
     arrived(1, r_bias1)
-    s_bias2[...] = r_bias1[...].reshape(256, 128).T.reshape(8, 16, 256)
-    mine = s_bias2.at[pl.ds(half * 4, 4)]
-    slot = r_bias2.at[:, pl.ds(pl.multiple_of(bj * 16, 16), 16), :]
-    exchange(2, bj, on_bj, lambda b: mine, slot)
+    turned = r_bias1[...].reshape(128, 128).T
+    for ih in range(2):
+        s_bias2[:, :, :, 128 * ih : 128 * ih + 128] = turned[64 * ih : 64 * ih + 64].reshape(4, 2, 8, 128)
+
+    def slot(branch, j):
+        return r_bias2.at[:, :, pl.ds(pl.multiple_of(branch * 64 + j * 8, 8), 8), :]
+
+    def pass_on(n, src, j, device):
+        pltpu.make_async_remote_copy(
+            src_ref=src, dst_ref=slot(core, j), send_sem=ssem.at[2], recv_sem=bsem.at[n],
+            device_id=device, device_id_type=MESH,
+        ).start()
+
+    sibling = {"branch": 1 - core}
+
+    @pl.loop(1, 8)
+    def _(d):
+        pass_on(d, s_bias2, gj, {"gj": lax.rem(gj + d, 8)})
+
+    pass_on(0, s_bias2, gj, sibling)
+    keep(2, s_bias2, slot(core, gj))
+
+    @pl.loop(1, 8)
+    def _(d):
+        j = lax.rem(gj + 8 - d, 8)
+        pltpu.make_async_copy(slot(core, j), slot(core, j), bsem.at[d]).wait()
+        pass_on(7 + d, slot(core, j), j, sibling)
 
     arrived(0, r_raw)
+    loads["scales"].wait()
     x = norm(r_raw[...].reshape(256, 256), scales[0:1, :])
     xs = split(x)
     q = split(mm(xs, weight(bq, columns=slice(0, 128))))
@@ -214,11 +249,14 @@
     for h in range(4):
         scores[h] = head_scores(k, q, h)
     ready("f", wf, bf)
-    arrived(2, r_bias2)
-    heads = [attend(scores[h] + r_bias2[h], vt, h) for h in range(4)]
+    arrived(2, s_bias2)
+    for d in range(8):
+        j = lax.rem(gj + 8 - d, 8)
+        pltpu.make_async_copy(slot(1 - core, j), slot(1 - core, j), bsem.at[7 + d if d else 0]).wait()
+    heads = [attend(scores[h] + r_bias2[h].reshape(256, 256), vt, h) for h in range(4)]
     att = gate[...] * jnp.concatenate(heads, axis=0).T
-    s_att[...] = att.reshape(16, 16, 128)
-    exchange(3, gi, on_gi, lambda g: s_att.at[g], r_att.at[gi])
+    s_att[...] = att.reshape(2, 16, 8, 128)
+    exchange(3, gi, on_gi, lambda g: s_att.at[:, g], r_att.at[gi])
     ready("v", wv, bv)
     ready("vf", wvf, bvf)
 
@@ -260,7 +298,7 @@
     s_al[0], s_al[1] = al[:, :128], al[:, 128:]
     for copy in loads["d"]:
         copy.wait()
-    factors = mm(split(norm(al, scales[3:4, :])), split(wd[...])).T
+    factors = mm(split(wd[...]), split(norm(al, scales[3:4, :])), NT)
     s_ab[...] = factors.reshape(2, 32, 128)
     exchange(5, bj, on_bj, lambda b: s_ab.at[0], r_a.at[bj])
 
@@ -341,9 +379,10 @@
     out_pair[...] = y.reshape(16, 16, 128)
 
     fifteen = pl.ds(0, 15)
-    for n, ref in ((0, r_raw), (1, r_bias1), (3, s_att), (4, s_col), (5, r_a), (12, s_c)):
+    for n, ref in ((1, r_bias1), (3, r_att), (4, s_col), (5, r_a), (12, s_c)):
         sent(n, ref.at[fifteen])
-    sent(2, r_bias2.at[:, pl.ds(0, 240), :])
+    sent(0, r_raw.at[:, fifteen])
+    sent(2, r_bias2.at[:, :, pl.ds(0, 120), :])
     for n, ref in ((7, s_al), (8, s_ta), (9, s_tb), (13, s_d)):
         sent(n, ref.at[:, pl.ds(0, 120), :])
     sent(10, r_ba.at[fifteen])
@@ -360,28 +399,34 @@
         return pltpu.VMEM(shape, dtype)
 
     widths = (
-        (256, 512), (256, 256), (256, 1024), (256, 256), (256, 1024), (1024, 256), (256, 64),
+        (256, 512), (256, 256), (256, 1024), (256, 256), (256, 1024), (1024, 256), (64, 256),
         (1024, 128), (128, 640), (128, 128),
     )
-    scratch = [vmem(*w) for w in widths] + [vmem(2, *w, dtype=BF16) for w in widths] + [
-        vmem(16, 128), vmem(16, 16, 128), vmem(8, 16, 256), vmem(4, 256, 256), vmem(16, 16, 256),
+    small = ((8, 2, 8, 256), (16, 16, 128), (4, 256), (3, 128), (8, 128))
+    scratch = [vmem(*w) for w in small + widths]
+    scratch += [vmem(2, *w, dtype=BF16) for w in widths if w != (64, 256)] + [
+        vmem(2, 8, 128), vmem(16, 8, 128), vmem(4, 2, 8, 256), vmem(4, 2, 128, 256), vmem(2, 16, 8, 256),
         vmem(256, 128), vmem(4, 256, 256),
-        vmem(16, 16, 128), vmem(16, 16, 128), vmem(2, 128, 128), vmem(16, 8, 256), vmem(16, 8, 256),
+        vmem(2, 16, 8, 128), vmem(16, 2, 8, 128), vmem(2, 128, 128), vmem(16, 8, 256), vmem(16, 8, 256),
         vmem(2, 128, 128), vmem(2, 128, 128), vmem(2, 32, 128), vmem(16, 32, 128), vmem(16, 32, 128),
         vmem(16, 16, 128), vmem(256, 128), vmem(2, 128, 128), vmem(2, 128, 128), vmem(2, 128, 128), vmem(2, 128, 128),
         vmem(8, 16, 256), vmem(8, 16, 256), vmem(16, 16, 256), vmem(8, 16, 256),
         vmem(16, 16, 128), vmem(16, 16, 128), vmem(2, 128, 128), vmem(2, 128, 128),
-        pltpu.SemaphoreType.DMA((13,)), pltpu.SemaphoreType.DMA((14,)), pltpu.SemaphoreType.DMA((14,)),
+        pltpu.SemaphoreType.DMA((19,)), pltpu.SemaphoreType.DMA((14,)), pltpu.SemaphoreType.DMA((14,)),
+        pltpu.SemaphoreType.DMA((15,)),
     ]
 
     def per_device(*args):
+        args = list(args)
+        args[0] = args[0].reshape(8, 2, 8, 256)
+        args[4], args[11] = args[4].T, args[11].T
         return pl.pallas_call(
             kernel,
             out_shape=(
-                jax.ShapeDtypeStruct((8, 16, 256), F32),
-                jax.ShapeDtypeStruct((16, 16, 128), F32),
+                pltpu.VMEM((8, 16, 256), F32),
+                pltpu.VMEM((16, 16, 128), F32),
             ),
-            in_specs=[pl.BlockSpec(memory_space=pltpu.VMEM)] * 5 + [pl.BlockSpec(memory_space=pl.ANY)] * 10,
+            in_specs=[pl.BlockSpec(memory_space=pl.ANY)] * 15,
             out_specs=(pl.BlockSpec(memory_space=pltpu.VMEM),) * 2,
             scratch_shapes=scratch,
             compiler_params=pltpu.CompilerParams(

time: 100 us -> 87.3 us (0.87)
  Pallas kernels: 94.8 us -> 85.3 us
  local copies, waits for them, and re-layouts: 4.47 us -> 1.31 us
    pallas_call x1, Pallas kernels: 94.8 us -> 85.3 us  [per_device(): pl.pallas_call(kernel, out_shape=(pltpu.VMEM((8, 16, 256), F32), pltpu.VM...]
    unnamed x8 -> x2, local copies, waits for them, and re-layouts: 4.47 us -> 1.31 us
where the time goes in v2:
time: 87.3 us
  Pallas kernels  85.3 us (98%)
  local copies, waits for them, and re-layouts  1.31 us (2%)
    pallas_call x1, Pallas kernels, per_device(): pl.pallas_call(kernel, out_shape=(pltpu.VMEM((8, 16, 256), F32), pltpu.VM...  85.3 us

profile of v2, /device:TPU:1, one launch (start us, length us, event | category | flops | bytes accessed | tf_op | source)
XLA Modules:
  0.0 87.3 jit_solution(10826238607101356015)
XLA Ops:
  0.6 85.3 %block.1 = (f32[8,16,256]{2,1,0:T(8,128)S(1)}, f32[16,16,128]{2,1,0:T(8,128)S(1)}) custom-call(f32[8,2,8,256]{3,2,1,0:T(8,128)} %bitcast.3, f32[16,16,128]{2,1,0:T(8,128)} %h_pair.1, f32[4,256]{1,0:T(4,128)} %h_scales.1, f32[3,128]{1,0:T(4,128)} %h_pgains.1, f32[8,128]{1,0:T(8,128)} %bitcast.5, f32[256,1024]{1,0:T(8,128)} %h_wq.1, f32[256,256]{1,0:T(8,128)} %h_wf.1, ...), custom_call_target="tpu_custom_call" | custom-call | tf_op jit(solution)/shard_map/block/pallas_call | solution.py:423
  85.9 0.7 copy.19
  86.6 0.7 copy.20

commit v3 on v2

--- a/solution.py
+++ b/solution.py
@@ -108,7 +108,7 @@
     bq, bf, bv, bvf, be, bs, bo, bt, bto,
     s_bias1, r_bias1, s_bias2, r_bias2, r_raw, gate, scores,
     s_att, r_att, first, s_col, r_col, s_al, r_al, s_ab, r_a, r_b,
-    pf, gout, s_ta, s_tb, r_ta, r_tb, s_ba, s_bb, r_ba, r_bb, s_c, r_c, s_d, r_d,
+    pf, gout, s_ta, s_tb, r_ta, r_tb, s_ba, s_bb, r_ba, r_bb, s_d, r_d,
     wsem, ssem, rsem, bsem,
 ):
     core, gi, gj = lax.axis_index("branch"), lax.axis_index("gi"), lax.axis_index("gj")
@@ -124,18 +124,35 @@
     def cross(g):
         return {"gi": g, "branch": gi // 8, "gj": gi % 8}
 
-    def each(count, me, one):
-        @pl.loop(1, count)
-        def _(d):
-            one(lax.rem(me + d, count))
+    gx, gy = gj // 2, gj % 2
+
+    def flip(bit, where):
+        return where if bit == 0 else 1 - where
+
+    def gi_peers():
+        steps = sorted(((dy, dz) for dy in range(2) for dz in range(8)), key=lambda s: -2 * s[0] - min(s[1], 8 - s[1]))
+        return [flip(dy, half) * 8 + (z + dz) % 8 for dy, dz in steps[:-1]]
+
+    def gj_peers():
+        steps = sorted(((dx, dy) for dx in range(4) for dy in range(2)), key=lambda s: -s[1] - min(s[0], 4 - s[0]))
+        return [((gx + dx) % 4 if dx else gx, flip(dy, gy)) for dx, dy in steps]
+
+    def bj_peers():
+        own = gj_peers()
+        every = [flip(dc, core) * 8 + px * 2 + py for px, py in own for dc in (1, 0)]
+        return every[:-1]
+
+    def each(peers, one):
+        for peer in peers:
+            one(peer)
 
     barrier = pltpu.get_barrier_semaphore()
 
     def greet(device):
         pl.semaphore_signal(barrier, inc=1, device_id=device, device_id_type=MESH)
 
-    each(16, gi, lambda g: greet(on_gi(g)))
-    each(16, bj, lambda b: greet(on_bj(b)))
+    each(gi_peers(), lambda g: greet(on_gi(g)))
+    each(bj_peers(), lambda b: greet(on_bj(b)))
 
     def load(n, src, dst):
         copy = pltpu.make_async_copy(src, dst, wsem.at[n])
@@ -188,8 +205,19 @@
         pltpu.make_async_copy(src, dst, rsem.at[n]).start()
 
     def exchange(n, me, device, src, dst):
+        peers = gi_peers() if device is on_gi else bj_peers()
+        each(peers, lambda peer: send(n, src(peer), dst, device(peer)))
         keep(n, src(me), dst)
-        each(16, me, lambda peer: send(n, src(peer), dst, device(peer)))
+
+    def far_first(one):
+        @pl.loop(0, 7)
+        def _(k):
+            there = (z + jnp.where(k % 2 == 1, 4 - (k + 1) // 2, 4 + k // 2)) % 8
+            one((1 - half) * 8 + there, False)
+            one(half * 8 + there, False)
+
+        one((1 - half) * 8 + z, False)
+        one(gi, True)
 
     def eight(ref, b):
         return ref.at[:, pl.ds(pl.multiple_of(b * 8, 8), 8), :]
@@ -209,6 +237,12 @@
     loads["hom"].wait()
     exchange(0, gi, on_gi, lambda g: hom.at[g % 8], r_raw.at[:, gi])
     ready("q", wq, bq)
+    value = hom[...].reshape(128, 256)
+    for n in range(2):
+        lanes = slice(128 * n, 128 * n + 128)
+        first[n] = value[:, lanes]
+        for p in range(16):
+            s_col[p, :, lanes] = first[n, pl.ds(p, 8, stride=16), :]
     arrived(1, r_bias1)
     turned = r_bias1[...].reshape(128, 128).T
     for ih in range(2):
@@ -225,18 +259,19 @@
 
     sibling = {"branch": 1 - core}
 
-    @pl.loop(1, 8)
-    def _(d):
-        pass_on(d, s_bias2, gj, {"gj": lax.rem(gj + d, 8)})
-
+    to = [(px * 2 + py) for px, py in gj_peers()]
+    steps = sorted(((dx, dy) for dx in range(4) for dy in range(2)), key=lambda s: -s[1] - min(s[0], 4 - s[0]))
+    senders = [((gx + 4 - dx) % 4 * 2 + flip(dy, gy)) for dx, dy in steps]
+    for d in range(7):
+        pass_on(d + 1, s_bias2, gj, {"gj": to[d]})
     pass_on(0, s_bias2, gj, sibling)
     keep(2, s_bias2, slot(core, gj))
-
-    @pl.loop(1, 8)
-    def _(d):
-        j = lax.rem(gj + 8 - d, 8)
-        pltpu.make_async_copy(slot(core, j), slot(core, j), bsem.at[d]).wait()
-        pass_on(7 + d, slot(core, j), j, sibling)
+    for d in range(7):
+        j = senders[d]
+        pltpu.make_async_copy(slot(core, j), slot(core, j), bsem.at[d + 1]).wait()
+        pass_on(8 + d, slot(core, j), j, sibling)
+
+    exchange(4, bj, on_bj, lambda b: s_col.at[b], r_col.at[bj])
 
     arrived(0, r_raw)
     loads["scales"].wait()
@@ -250,34 +285,35 @@
         scores[h] = head_scores(k, q, h)
     ready("f", wf, bf)
     arrived(2, s_bias2)
-    for d in range(8):
-        j = lax.rem(gj + 8 - d, 8)
-        pltpu.make_async_copy(slot(1 - core, j), slot(1 - core, j), bsem.at[7 + d if d else 0]).wait()
+    for n, j in enumerate([gj] + senders[:7]):
+        pltpu.make_async_copy(slot(1 - core, j), slot(1 - core, j), bsem.at[7 + n if n else 0]).wait()
     heads = [attend(scores[h] + r_bias2[h].reshape(256, 256), vt, h) for h in range(4)]
     att = gate[...] * jnp.concatenate(heads, axis=0).T
-    s_att[...] = att.reshape(2, 16, 8, 128)
-    exchange(3, gi, on_gi, lambda g: s_att.at[:, g], r_att.at[gi])
+    s_att[:, 0, :] = att
+    seat = r_att.at[half, pl.ds(bj * 8 + z, 1)]
+
+    def to_columns(g, mine):
+        for px, py in gj_peers():
+            for c in (1, 0):
+                there = flip(c, core)
+                src = s_att.at[pl.ds(there * 128 + g * 8 + px * 2 + py, 1)]
+                if mine and c == 0 and py is gy and (px is gx):
+                    keep(3, src, seat)
+                else:
+                    send(3, src, seat, {"branch": there, "gi": g, "gj": px * 2 + py})
+
+    far_first(to_columns)
     ready("v", wv, bv)
     ready("vf", wvf, bvf)
-
-    arrived(3, r_att)
-    a = r_att[...].reshape(256, 128)
-    value = (
-        hom[...].reshape(128, 256)
-        + mm(split(a[:128]), weight(bf, slice(0, 128)))
-        + mm(split(a[128:]), weight(bf, slice(128, 256)))
-    )
-    for n in range(2):
-        lanes = slice(128 * n, 128 * n + 128)
-        first[n] = value[:, lanes]
-        for p in range(16):
-            s_col[p, :, lanes] = first[n, pl.ds(p, 8, stride=16), :]
-    exchange(4, bj, on_bj, lambda b: s_col.at[b], r_col.at[bj])
     ready("e", we, be)
     ready("s", ws, bs)
 
+    arrived(3, r_att)
+    col = mm(split(r_att[0, :, 0, :]), weight(bf, slice(0, 128)))
+    col += mm(split(r_att[1, :, 0, :]), weight(bf, slice(128, 256)))
+    first[0], first[1] = col[:, :128], col[:, 128:]
     arrived(4, r_col)
-    col = r_col[...].reshape(128, 256)
+    col = r_col[...].reshape(128, 256) + jnp.concatenate([first[0], first[1]], axis=1)
     xs = split(norm(col, scales[1:2, :]))
     pieces = []
     for n in range(2):
@@ -300,20 +336,18 @@
         copy.wait()
     factors = mm(split(wd[...]), split(norm(al, scales[3:4, :])), NT)
     s_ab[...] = factors.reshape(2, 32, 128)
+
+    each(gi_peers(), lambda g: send(6, s_ab.at[1], r_b.at[bj], cross(g)))
+
+    @pl.when(gi == bj)
+    def _():
+        keep(6, s_ab.at[1], r_b.at[bj])
+
+    @pl.when(gi != bj)
+    def _():
+        send(6, s_ab.at[1], r_b.at[bj], cross(gi))
+
     exchange(5, bj, on_bj, lambda b: s_ab.at[0], r_a.at[bj])
-
-    @pl.loop(0, 16)
-    def _(d):
-        g = lax.rem(gi + d, 16)
-        stays = jnp.logical_and(g == gi, gi == bj)
-
-        @pl.when(stays)
-        def _():
-            keep(6, s_ab.at[1], r_b.at[bj])
-
-        @pl.when(jnp.logical_not(stays))
-        def _():
-            send(6, s_ab.at[1], r_b.at[bj], cross(g))
 
     exchange(7, bj, on_bj, lambda b: eight(s_al, b), eight(r_al, bj))
     ready("o", wo, bo)
@@ -354,40 +388,61 @@
     arrived(9, r_tb)
     regroup(r_tb, s_bb)
     keep(11, s_bb.at[z], r_bb.at[z])
-    each(8, z, lambda other: send(11, s_bb.at[other], r_bb.at[z], on_gi(half * 8 + other)))
+    for dz in (4, 3, 5, 2, 6, 1, 7):
+        other = (z + dz) % 8
+        send(11, s_bb.at[other], r_bb.at[z], on_gi(half * 8 + other))
     arrived(10, r_ba)
     arrived(11, r_bb)
     x = mm(split(r_ba[...].reshape(256, 256)), split(r_bb[...].reshape(128, 256)), NT)
-    s_c[...] = x.reshape(16, 16, 128)
-    exchange(12, gi, on_gi, lambda g: s_c.at[g], r_c.at[gi])
+    x = x.reshape(16, 2, 8, 128)
+    for ih in range(2):
+        s_d[ih, :, 0, :] = swap_blocks(x[:, ih], 3, 4).reshape(128, 128)
+    place = r_d.at[:, pl.ds(bj * 8 + z, 1)]
+
+    def to_pairs(g, mine):
+        for px, py in gj_peers():
+            src = s_d.at[:, pl.ds(g * 8 + px * 2 + py, 1)]
+            device = {"branch": half, "gi": g, "gj": px * 2 + py}
+            if mine and py is gy and px is gx:
+
+                @pl.when(core == half)
+                def _():
+                    keep(13, src, place)
+
+                @pl.when(core != half)
+                def _():
+                    send(13, src, place, device)
+            else:
+                send(13, src, place, device)
+
+    far_first(to_pairs)
 
     arrived(7, r_al)
     for row in range(8):
         for n in range(2):
             out_al[row, :, 128 * n : 128 * n + 128] = r_al[n, pl.ds(row, 16, stride=8), :]
 
-    arrived(12, r_c)
-    for hh in range(2):
-        for ih in range(2):
-            block = swap_blocks(r_c[8 * hh : 8 * hh + 8, 8 * ih : 8 * ih + 8, :], 3, 4)
-            for c in range(8):
-                s_d[ih, pl.ds(64 * hh + c, 8, stride=8), :] = block[c]
-    exchange(13, bj, on_bj, lambda b: eight(s_d, b), eight(r_d, bj))
     arrived(13, r_d)
-    x = norm(jnp.concatenate([r_d[0].T, r_d[1].T], axis=0), pgains[2:3, :])
+    x = norm(jnp.concatenate([r_d[0, :, 0, :].T, r_d[1, :, 0, :].T], axis=0), pgains[2:3, :])
     y = pf[...].reshape(256, 128) + gout[...] * mm(split(x), weight(bto))
     out_pair[...] = y.reshape(16, 16, 128)
 
     fifteen = pl.ds(0, 15)
-    for n, ref in ((1, r_bias1), (3, r_att), (4, s_col), (5, r_a), (12, s_c)):
+    for n, ref in ((1, r_bias1), (4, s_col), (5, r_a)):
         sent(n, ref.at[fifteen])
     sent(0, r_raw.at[:, fifteen])
     sent(2, r_bias2.at[:, :, pl.ds(0, 120), :])
-    for n, ref in ((7, s_al), (8, s_ta), (9, s_tb), (13, s_d)):
+    for n, ref in ((7, s_al), (8, s_ta), (9, s_tb)):
         sent(n, ref.at[:, pl.ds(0, 120), :])
     sent(10, r_ba.at[fifteen])
     sent(11, r_bb.at[pl.ds(0, 7)])
     sent(6, r_b.at[fifteen])
+    sent(3, s_att.at[pl.ds(0, 255)])
+    sent(13, s_d.at[:, pl.ds(0, 127)])
+
+    @pl.when(core != half)
+    def _():
+        sent(13, s_d.at[:, pl.ds(0, 1)])
 
     @pl.when(gi != bj)
     def _():
@@ -407,11 +462,11 @@
     scratch += [vmem(2, *w, dtype=BF16) for w in widths if w != (64, 256)] + [
         vmem(2, 8, 128), vmem(16, 8, 128), vmem(4, 2, 8, 256), vmem(4, 2, 128, 256), vmem(2, 16, 8, 256),
         vmem(256, 128), vmem(4, 256, 256),
-        vmem(2, 16, 8, 128), vmem(16, 2, 8, 128), vmem(2, 128, 128), vmem(16, 8, 256), vmem(16, 8, 256),
+        vmem(256, 1, 128), vmem(2, 128, 1, 128), vmem(2, 128, 128), vmem(16, 8, 256), vmem(16, 8, 256),
         vmem(2, 128, 128), vmem(2, 128, 128), vmem(2, 32, 128), vmem(16, 32, 128), vmem(16, 32, 128),
         vmem(16, 16, 128), vmem(256, 128), vmem(2, 128, 128), vmem(2, 128, 128), vmem(2, 128, 128), vmem(2, 128, 128),
         vmem(8, 16, 256), vmem(8, 16, 256), vmem(16, 16, 256), vmem(8, 16, 256),
-        vmem(16, 16, 128), vmem(16, 16, 128), vmem(2, 128, 128), vmem(2, 128, 128),
+        vmem(2, 128, 1, 128), vmem(2, 128, 1, 128),
         pltpu.SemaphoreType.DMA((19,)), pltpu.SemaphoreType.DMA((14,)), pltpu.SemaphoreType.DMA((14,)),
         pltpu.SemaphoreType.DMA((15,)),
     ]

time: 87.3 us -> 78.9 us (0.904)
  Pallas kernels: 85.3 us -> 76.9 us
    pallas_call x1, Pallas kernels: 85.3 us -> 76.9 us  [per_device(): pl.pallas_call(kernel, out_shape=(pltpu.VMEM((8, 16, 256), F32), pltpu.VM...]
where the time goes in v3:
time: 78.9 us; the launch traced here: 78.8 us
  Pallas kernels  76.9 us (97%)
  local copies, waits for them, and re-layouts  1.31 us (2%)
    pallas_call x1, Pallas kernels, per_device(): pl.pallas_call(kernel, out_shape=(pltpu.VMEM((8, 16, 256), F32), pltpu.VM...  76.9 us

profile of v3, /device:TPU:1, one launch (start us, length us, event | category | flops | bytes accessed | tf_op | source)
XLA Modules:
  0.0 78.8 jit_solution(8244409119127703467)
XLA Ops:
  0.6 76.9 %block.1 = (f32[8,16,256]{2,1,0:T(8,128)S(1)}, f32[16,16,128]{2,1,0:T(8,128)S(1)}) custom-call(f32[8,2,8,256]{3,2,1,0:T(8,128)} %bitcast.3, f32[16,16,128]{2,1,0:T(8,128)} %h_pair.1, f32[4,256]{1,0:T(4,128)} %h_scales.1, f32[3,128]{1,0:T(4,128)} %h_pgains.1, f32[8,128]{1,0:T(8,128)} %bitcast.5, f32[256,1024]{1,0:T(8,128)} %h_wq.1, f32[256,256]{1,0:T(8,128)} %h_wf.1, ...), custom_call_target="tpu_custom_call" | custom-call | tf_op jit(solution)/shard_map/block/pallas_call | solution.py:478
  77.5 0.7 copy.19
  78.2 0.7 copy.20

commit v4 on v3

--- a/solution.py
+++ b/solution.py
@@ -109,7 +109,7 @@
     s_bias1, r_bias1, s_bias2, r_bias2, r_raw, gate, scores,
     s_att, r_att, first, s_col, r_col, s_al, r_al, s_ab, r_a, r_b,
     pf, gout, s_ta, s_tb, r_ta, r_tb, s_ba, s_bb, r_ba, r_bb, s_d, r_d,
-    wsem, ssem, rsem, bsem,
+    wsem, ssem, rsem, bsem, csem,
 ):
     core, gi, gj = lax.axis_index("branch"), lax.axis_index("gi"), lax.axis_index("gj")
     bj = core * 8 + gj
@@ -382,38 +382,64 @@
                 block = jnp.stack([src[ih, pl.ds(64 * bh + c, 8, stride=8), :] for c in range(8)])
                 dst[:, 8 * ih : 8 * ih + 8, 128 * bh : 128 * bh + 128] = swap_blocks(block, 3, 4)
 
+    paired = core == half
+
+    def to_channels(one):
+        for dz in (4, 3, 5, 2, 6, 1, 7):
+            one((z + dz) % 8)
+
+        @pl.when(core != half)
+        def _():
+            one(z)
+
+    def left(there):
+        pltpu.make_async_remote_copy(
+            src_ref=s_ba.at[there], dst_ref=r_ba.at[gi], send_sem=ssem.at[10], recv_sem=csem.at[gi],
+            device_id={"gi": core * 8 + there}, device_id_type=MESH,
+        ).start()
+
+    def right(there):
+        send(11, s_bb.at[there], r_bb.at[z], {"gi": core * 8 + there, "branch": half})
+
     arrived(8, r_ta)
     regroup(r_ta, s_ba)
-    exchange(10, gi, on_gi, lambda g: s_ba.at[g % 8], r_ba.at[gi])
+    to_channels(left)
+
+    @pl.when(paired)
+    def _():
+        pltpu.make_async_copy(s_ba.at[z], r_ba.at[gi], csem.at[gi]).start()
+
     arrived(9, r_tb)
     regroup(r_tb, s_bb)
-    keep(11, s_bb.at[z], r_bb.at[z])
-    for dz in (4, 3, 5, 2, 6, 1, 7):
-        other = (z + dz) % 8
-        send(11, s_bb.at[other], r_bb.at[z], on_gi(half * 8 + other))
-    arrived(10, r_ba)
+    to_channels(right)
+
+    @pl.when(paired)
+    def _():
+        keep(11, s_bb.at[z], r_bb.at[z])
+        for dy in range(2):
+            for dz in (0, 1, 7, 2, 6, 3, 5, 4):
+                g = flip(dy, half) * 8 + (z + dz) % 8
+                pltpu.make_async_copy(r_ba.at[g], r_ba.at[g], csem.at[g]).wait()
+                send(10, r_ba.at[g], r_ba.at[g], sibling)
+
+    @pl.when(jnp.logical_not(paired))
+    def _():
+        arrived(10, r_ba)
+
     arrived(11, r_bb)
     x = mm(split(r_ba[...].reshape(256, 256)), split(r_bb[...].reshape(128, 256)), NT)
     x = x.reshape(16, 2, 8, 128)
     for ih in range(2):
         s_d[ih, :, 0, :] = swap_blocks(x[:, ih], 3, 4).reshape(128, 128)
-    place = r_d.at[:, pl.ds(bj * 8 + z, 1)]
+    place = r_d.at[:, pl.ds((half * 8 + gj) * 8 + z, 1)]
 
     def to_pairs(g, mine):
         for px, py in gj_peers():
             src = s_d.at[:, pl.ds(g * 8 + px * 2 + py, 1)]
-            device = {"branch": half, "gi": g, "gj": px * 2 + py}
             if mine and py is gy and px is gx:
-
-                @pl.when(core == half)
-                def _():
-                    keep(13, src, place)
-
-                @pl.when(core != half)
-                def _():
-                    send(13, src, place, device)
+                keep(13, src, place)
             else:
-                send(13, src, place, device)
+                send(13, src, place, {"gi": g, "gj": px * 2 + py})
 
     far_first(to_pairs)
 
@@ -434,15 +460,21 @@
     sent(2, r_bias2.at[:, :, pl.ds(0, 120), :])
     for n, ref in ((7, s_al), (8, s_ta), (9, s_tb)):
         sent(n, ref.at[:, pl.ds(0, 120), :])
-    sent(10, r_ba.at[fifteen])
+    sent(10, r_ba.at[pl.ds(0, 7)])
+
+    @pl.when(paired)
+    def _():
+        sent(10, r_ba)
+
+    @pl.when(jnp.logical_not(paired))
+    def _():
+        sent(10, r_ba.at[pl.ds(0, 1)])
+        sent(11, r_bb.at[pl.ds(0, 1)])
+
     sent(11, r_bb.at[pl.ds(0, 7)])
     sent(6, r_b.at[fifteen])
     sent(3, s_att.at[pl.ds(0, 255)])
     sent(13, s_d.at[:, pl.ds(0, 127)])
-
-    @pl.when(core != half)
-    def _():
-        sent(13, s_d.at[:, pl.ds(0, 1)])
 
     @pl.when(gi != bj)
     def _():
@@ -468,7 +500,7 @@
         vmem(8, 16, 256), vmem(8, 16, 256), vmem(16, 16, 256), vmem(8, 16, 256),
         vmem(2, 128, 1, 128), vmem(2, 128, 1, 128),
         pltpu.SemaphoreType.DMA((19,)), pltpu.SemaphoreType.DMA((14,)), pltpu.SemaphoreType.DMA((14,)),
-        pltpu.SemaphoreType.DMA((15,)),
+        pltpu.SemaphoreType.DMA((15,)), pltpu.SemaphoreType.DMA((16,)),
     ]
 
     def per_device(*args):

time: 78.9 us -> 76.8 us (0.973)
  Pallas kernels: 76.9 us -> 74.7 us
    pallas_call x1, Pallas kernels: 76.9 us -> 74.7 us  [per_device(): pl.pallas_call(kernel, out_shape=(pltpu.VMEM((8, 16, 256), F32), pltpu.VM...]
where the time goes in v4:
time: 76.8 us; the launch traced here: 76.7 us
  Pallas kernels  74.7 us (97%)
  local copies, waits for them, and re-layouts  1.31 us (2%)
    pallas_call x1, Pallas kernels, per_device(): pl.pallas_call(kernel, out_shape=(pltpu.VMEM((8, 16, 256), F32), pltpu.VM...  74.7 us

profile of v4, /device:TPU:1, one launch (start us, length us, event | category | flops | bytes accessed | tf_op | source)
XLA Modules:
  0.0 76.7 jit_solution(9022051793732794081)
XLA Ops:
  0.6 74.7 %block.1 = (f32[8,16,256]{2,1,0:T(8,128)S(1)}, f32[16,16,128]{2,1,0:T(8,128)S(1)}) custom-call(f32[8,2,8,256]{3,2,1,0:T(8,128)} %bitcast.3, f32[16,16,128]{2,1,0:T(8,128)} %h_pair.1, f32[4,256]{1,0:T(4,128)} %h_scales.1, f32[3,128]{1,0:T(4,128)} %h_pgains.1, f32[8,128]{1,0:T(8,128)} %bitcast.5, f32[256,1024]{1,0:T(8,128)} %h_wq.1, f32[256,256]{1,0:T(8,128)} %h_wf.1, ...), custom_call_target="tpu_custom_call" | custom-call | tf_op jit(solution)/shard_map/block/pallas_call | solution.py:510
  75.4 0.7 copy.19
  76.0 0.7 copy.20

commit v5 on v4

--- a/solution.py
+++ b/solution.py
@@ -106,7 +106,7 @@
     hom, pair, scales, pgains, wb,
     wq, wf, wv, wvf, we, ws, wd, wo, wt, wto,
     bq, bf, bv, bvf, be, bs, bo, bt, bto,
-    s_bias1, r_bias1, s_bias2, r_bias2, r_raw, gate, scores,
+    s_bias1, r_bias1, s_bias2, r_bias2, r_raw, gate, scores, turned_v,
     s_att, r_att, first, s_col, r_col, s_al, r_al, s_ab, r_a, r_b,
     pf, gout, s_ta, s_tb, r_ta, r_tb, s_ba, s_bb, r_ba, r_bb, s_d, r_d,
     wsem, ssem, rsem, bsem, csem,
@@ -266,27 +266,27 @@
         pass_on(d + 1, s_bias2, gj, {"gj": to[d]})
     pass_on(0, s_bias2, gj, sibling)
     keep(2, s_bias2, slot(core, gj))
+    arrived(0, r_raw)
+    loads["scales"].wait()
+    x = norm(r_raw[...].reshape(256, 256), scales[0:1, :])
+    p = mm(split(x), weight(bq))
+    q, k, vt = split(p[:, :128]), split(p[:, 128:256]), split(p[:, 256:384].T)
+    gate[...] = jax.nn.sigmoid(p[:, 384:])
+    for h in range(4):
+        scores[h] = head_scores(k, q, h)
+    turned_v[0], turned_v[1] = vt
+
     for d in range(7):
         j = senders[d]
         pltpu.make_async_copy(slot(core, j), slot(core, j), bsem.at[d + 1]).wait()
         pass_on(8 + d, slot(core, j), j, sibling)
 
     exchange(4, bj, on_bj, lambda b: s_col.at[b], r_col.at[bj])
-
-    arrived(0, r_raw)
-    loads["scales"].wait()
-    x = norm(r_raw[...].reshape(256, 256), scales[0:1, :])
-    xs = split(x)
-    q = split(mm(xs, weight(bq, columns=slice(0, 128))))
-    k = split(mm(xs, weight(bq, columns=slice(128, 256))))
-    vt = split(mm(xs, weight(bq, columns=slice(256, 384))).T)
-    gate[...] = jax.nn.sigmoid(mm(xs, weight(bq, columns=slice(384, 512))))
-    for h in range(4):
-        scores[h] = head_scores(k, q, h)
     ready("f", wf, bf)
     arrived(2, s_bias2)
     for n, j in enumerate([gj] + senders[:7]):
         pltpu.make_async_copy(slot(1 - core, j), slot(1 - core, j), bsem.at[7 + n if n else 0]).wait()
+    vt = turned_v[0], turned_v[1]
     heads = [attend(scores[h] + r_bias2[h].reshape(256, 256), vt, h) for h in range(4)]
     att = gate[...] * jnp.concatenate(heads, axis=0).T
     s_att[:, 0, :] = att
@@ -315,13 +315,11 @@
     arrived(4, r_col)
     col = r_col[...].reshape(128, 256) + jnp.concatenate([first[0], first[1]], axis=1)
     xs = split(norm(col, scales[1:2, :]))
+    p = mm(xs, weight(bv))
     pieces = []
     for n in range(2):
-        lanes = [slice(256 * b + 128 * n, 256 * b + 128 * n + 128) for b in range(4)]
-        q = split(mm(xs, weight(bv, columns=lanes[0])))
-        k = split(mm(xs, weight(bv, columns=lanes[1])))
-        vt = split(mm(xs, weight(bv, columns=lanes[2])).T)
-        g = jax.nn.sigmoid(mm(xs, weight(bv, columns=lanes[3])))
+        q, k, v, g = (p[:, 256 * b + 128 * n : 256 * b + 128 * n + 128] for b in range(4))
+        q, k, vt, g = split(q), split(k), split(v.T), jax.nn.sigmoid(g)
         heads = [attend(head_scores(k, q, h), vt, h) for h in range(4)]
         pieces.append(g * jnp.concatenate(heads, axis=0).T)
     second = (
@@ -366,7 +364,8 @@
         rows = slice(8 * n, 8 * n + 8)
         pf[:, rows, :] = pair[:, rows, :] + updates[n]
     xs = split(norm(pf[...].reshape(256, 128), pgains[1:2, :]))
-    r = [mm(xs, weight(bt, columns=slice(128 * n, 128 * n + 128))) for n in range(5)]
+    p = mm(xs, weight(bt))
+    r = [p[:, 128 * n : 128 * n + 128] for n in range(5)]
     ta, tb = jax.nn.sigmoid(r[1]) * r[0], jax.nn.sigmoid(r[3]) * r[2]
     for n in range(2):
         s_ta[n] = ta[128 * n : 128 * n + 128].T
@@ -493,7 +492,7 @@
     scratch = [vmem(*w) for w in small + widths]
     scratch += [vmem(2, *w, dtype=BF16) for w in widths if w != (64, 256)] + [
         vmem(2, 8, 128), vmem(16, 8, 128), vmem(4, 2, 8, 256), vmem(4, 2, 128, 256), vmem(2, 16, 8, 256),
-        vmem(256, 128), vmem(4, 256, 256),
+        vmem(256, 128), vmem(4, 256, 256), vmem(2, 128, 256, dtype=BF16),
         vmem(256, 1, 128), vmem(2, 128, 1, 128), vmem(2, 128, 128), vmem(16, 8, 256), vmem(16, 8, 256),
         vmem(2, 128, 128), vmem(2, 128, 128), vmem(2, 32, 128), vmem(16, 32, 128), vmem(16, 32, 128),
         vmem(16, 16, 128), vmem(256, 128), vmem(2, 128, 128), vmem(2, 128, 128), vmem(2, 128, 128), vmem(2, 128, 128),

time: 76.8 us -> 76.3 us (level)
  no operation moved by 1% of the time
where the time goes in v5:
time: 76.3 us; the launch traced here: 76.2 us
  Pallas kernels  74.3 us (97%)
  local copies, waits for them, and re-layouts  1.31 us (2%)
    pallas_call x1, Pallas kernels, per_device(): pl.pallas_call(kernel, out_shape=(pltpu.VMEM((8, 16, 256), F32), pltpu.VM...  74.3 us

profile of v5, /device:TPU:1, one launch (start us, length us, event | category | flops | bytes accessed | tf_op | source)
XLA Modules:
  0.0 76.2 jit_solution(8026857692221691613)
XLA Ops:
  0.6 74.3 %block.1 = (f32[8,16,256]{2,1,0:T(8,128)S(1)}, f32[16,16,128]{2,1,0:T(8,128)S(1)}) custom-call(f32[8,2,8,256]{3,2,1,0:T(8,128)} %bitcast.3, f32[16,16,128]{2,1,0:T(8,128)} %h_pair.1, f32[4,256]{1,0:T(4,128)} %h_scales.1, f32[3,128]{1,0:T(4,128)} %h_pgains.1, f32[8,128]{1,0:T(8,128)} %bitcast.5, f32[256,1024]{1,0:T(8,128)} %h_wq.1, f32[256,256]{1,0:T(8,128)} %h_wf.1, ...), custom_call_target="tpu_custom_call" | custom-call | tf_op jit(solution)/shard_map/block/pallas_call | solution.py:509
  74.9 0.7 copy.19
  75.6 0.7 copy.20

commit v6 on v5

--- a/solution.py
+++ b/solution.py
@@ -364,16 +364,17 @@
         rows = slice(8 * n, 8 * n + 8)
         pf[:, rows, :] = pair[:, rows, :] + updates[n]
     xs = split(norm(pf[...].reshape(256, 128), pgains[1:2, :]))
-    p = mm(xs, weight(bt))
-    r = [p[:, 128 * n : 128 * n + 128] for n in range(5)]
-    ta, tb = jax.nn.sigmoid(r[1]) * r[0], jax.nn.sigmoid(r[3]) * r[2]
+    p = mm(xs, weight(bt, columns=slice(0, 256)))
+    factor = jax.nn.sigmoid(p[:, 128:]) * p[:, :128]
     for n in range(2):
-        s_ta[n] = ta[128 * n : 128 * n + 128].T
-        s_tb[n] = tb[128 * n : 128 * n + 128].T
-    gout[...] = jax.nn.sigmoid(r[4])
-
+        s_ta[n] = factor[128 * n : 128 * n + 128].T
     exchange(8, bj, on_bj, lambda b: eight(s_ta, b), eight(r_ta, bj))
+    p = mm(xs, weight(bt, columns=slice(256, 512)))
+    factor = jax.nn.sigmoid(p[:, 128:]) * p[:, :128]
+    for n in range(2):
+        s_tb[n] = factor[128 * n : 128 * n + 128].T
     exchange(9, bj, on_bj, lambda b: eight(s_tb, b), eight(r_tb, bj))
+    gout[...] = jax.nn.sigmoid(mm(xs, weight(bt, columns=slice(512, 640))))
 
     def regroup(src, dst):
         for ih in range(2):
@@ -419,17 +420,12 @@
             for dz in (0, 1, 7, 2, 6, 3, 5, 4):
                 g = flip(dy, half) * 8 + (z + dz) % 8
                 pltpu.make_async_copy(r_ba.at[g], r_ba.at[g], csem.at[g]).wait()
-                send(10, r_ba.at[g], r_ba.at[g], sibling)
-
-    @pl.when(jnp.logical_not(paired))
-    def _():
-        arrived(10, r_ba)
+                pltpu.make_async_remote_copy(
+                    src_ref=r_ba.at[g], dst_ref=r_ba.at[g], send_sem=ssem.at[10], recv_sem=rsem.at[10 + 4 * dy],
+                    device_id=sibling, device_id_type=MESH,
+                ).start()
 
     arrived(11, r_bb)
-    x = mm(split(r_ba[...].reshape(256, 256)), split(r_bb[...].reshape(128, 256)), NT)
-    x = x.reshape(16, 2, 8, 128)
-    for ih in range(2):
-        s_d[ih, :, 0, :] = swap_blocks(x[:, ih], 3, 4).reshape(128, 128)
     place = r_d.at[:, pl.ds((half * 8 + gj) * 8 + z, 1)]
 
     def to_pairs(g, mine):
@@ -440,17 +436,29 @@
             else:
                 send(13, src, place, {"gi": g, "gj": px * 2 + py})
 
-    far_first(to_pairs)
+    rights = split(r_bb[...].reshape(128, 256))
+    for dy in range(2):
+        there = flip(dy, half)
+        rows = r_ba.at[pl.ds(there * 8, 8)]
+
+        @pl.when(jnp.logical_not(paired))
+        def _():
+            arrived(10 + 4 * dy, rows)
+
+        x = mm(split(rows[...].reshape(128, 256)), rights, NT).reshape(8, 2, 8, 128)
+        for ih in range(2):
+            s_d[ih, pl.ds(there * 64, 64), 0, :] = swap_blocks(x[:, ih], 3, 4).reshape(64, 128)
+
+        @pl.loop(0, 7)
+        def _(k):
+            to_pairs(there * 8 + (z + jnp.where(k % 2 == 1, 4 - (k + 1) // 2, 4 + k // 2)) % 8, False)
+
+        to_pairs(there * 8 + z, dy == 0)
 
     arrived(7, r_al)
     for row in range(8):
         for n in range(2):
             out_al[row, :, 128 * n : 128 * n + 128] = r_al[n, pl.ds(row, 16, stride=8), :]
-
-    arrived(13, r_d)
-    x = norm(jnp.concatenate([r_d[0, :, 0, :].T, r_d[1, :, 0, :].T], axis=0), pgains[2:3, :])
-    y = pf[...].reshape(256, 128) + gout[...] * mm(split(x), weight(bto))
-    out_pair[...] = y.reshape(16, 16, 128)
 
     fifteen = pl.ds(0, 15)
     for n, ref in ((1, r_bias1), (4, s_col), (5, r_a)):
@@ -473,11 +481,17 @@
     sent(11, r_bb.at[pl.ds(0, 7)])
     sent(6, r_b.at[fifteen])
     sent(3, s_att.at[pl.ds(0, 255)])
+
+    @pl.when(gi != bj)
+    def _():
+        sent(6, r_b.at[pl.ds(0, 1)])
+
+    arrived(13, r_d)
+    x = norm(jnp.concatenate([r_d[0, :, 0, :].T, r_d[1, :, 0, :].T], axis=0), pgains[2:3, :])
+    y = pf[...].reshape(256, 128) + gout[...] * mm(split(x), weight(bto))
+    out_pair[...] = y.reshape(16, 16, 128)
+
     sent(13, s_d.at[:, pl.ds(0, 127)])
-
-    @pl.when(gi != bj)
-    def _():
-        sent(6, r_b.at[pl.ds(0, 1)])
 
 
 def solution(mesh):
@@ -498,7 +512,7 @@
         vmem(16, 16, 128), vmem(256, 128), vmem(2, 128, 128), vmem(2, 128, 128), vmem(2, 128, 128), vmem(2, 128, 128),
         vmem(8, 16, 256), vmem(8, 16, 256), vmem(16, 16, 256), vmem(8, 16, 256),
         vmem(2, 128, 1, 128), vmem(2, 128, 1, 128),
-        pltpu.SemaphoreType.DMA((19,)), pltpu.SemaphoreType.DMA((14,)), pltpu.SemaphoreType.DMA((14,)),
+        pltpu.SemaphoreType.DMA((19,)), pltpu.SemaphoreType.DMA((14,)), pltpu.SemaphoreType.DMA((15,)),
         pltpu.SemaphoreType.DMA((15,)), pltpu.SemaphoreType.DMA((16,)),
     ]
 

time: 76.3 us -> 75.3 us (0.987)
  Pallas kernels: 74.3 us -> 72.9 us
    pallas_call x1, Pallas kernels: 74.3 us -> 72.9 us  [per_device(): pl.pallas_call(kernel, out_shape=(pltpu.VMEM((8, 16, 256), F32), pltpu.VM...]
where the time goes in v6:
time: 75.3 us; the launch traced here: 74.9 us
  Pallas kernels  72.9 us (97%)
  local copies, waits for them, and re-layouts  1.31 us (2%)
    pallas_call x1, Pallas kernels, per_device(): pl.pallas_call(kernel, out_shape=(pltpu.VMEM((8, 16, 256), F32), pltpu.VM...  72.9 us

profile of v6, /device:TPU:1, one launch (start us, length us, event | category | flops | bytes accessed | tf_op | source)
XLA Modules:
  0.0 74.9 jit_solution(8532428458109039953)
XLA Ops:
  0.6 72.9 %block.1 = (f32[8,16,256]{2,1,0:T(8,128)S(1)}, f32[16,16,128]{2,1,0:T(8,128)S(1)}) custom-call(f32[8,2,8,256]{3,2,1,0:T(8,128)} %bitcast.3, f32[16,16,128]{2,1,0:T(8,128)} %h_pair.1, f32[4,256]{1,0:T(4,128)} %h_scales.1, f32[3,128]{1,0:T(4,128)} %h_pgains.1, f32[8,128]{1,0:T(8,128)} %bitcast.5, f32[256,1024]{1,0:T(8,128)} %h_wq.1, f32[256,256]{1,0:T(8,128)} %h_wf.1, ...), custom_call_target="tpu_custom_call" | custom-call | tf_op jit(solution)/shard_map/block/pallas_call | solution.py:523
  73.5 0.7 copy.19
  74.2 0.7 copy.20
